TPU v7x, 32 devices: a whole 2x2x4 slice. The times are simulated.
32 devices in a mesh: dp: 8 (over y, x, core), ffn: 4 (over z).
Axes of the slice: x: 2, y: 2, z: 4, core: 2. Of those that a mesh axis runs over, the one named last changes fastest.
Arguments:
- layer_activations: bfloat16 [64, 512, 768], P(('dp', 'ffn')), may hold values from -6 to 6
- token_counts_each: int32 [64], P(('dp', 'ffn')), may hold values from 64 to 512, as said below
- attention_triple_matrix: bfloat16 [768, 2304], P('dp', 'ffn'), may hold values from -0.21875 to 0.21875
- attention_final_matrix: bfloat16 [768, 768], P('dp', 'ffn'), may hold values from -1.75 to 1.75
- feedfwd_expand_matrix: bfloat16 [768, 3072], P('dp', 'ffn'), may hold values from -0.21875 to 0.21875
- feedfwd_expand_offset: bfloat16 [3072], P('ffn'), may hold values from -3 to 3
- feedfwd_contract_matrix: bfloat16 [3072, 768], P('ffn', 'dp'), may hold values from -0.109375 to 0.109375
- layernorm_scales: bfloat16 [2, 768], P(None, 'dp'), may hold values from 0.25 to 1.75
- offset_vectors: bfloat16 [6, 768], P(None, 'dp'), may hold values from -2 to 2
- learned_gate_scores: bfloat16 [512, 512], P('dp', 'ffn'), may hold values from -5 to 5
- fixed_jitter_matrix: bfloat16 [512, 512], P('dp', 'ffn'), may hold values from -1 to 1
- relaxation_heat: float32 [1], replicated, may hold values from 0.67 to 1
- loss_grad_result: bfloat16 [64, 512, 768], P(('dp', 'ffn')), may hold values from -6 to 6
Outputs:
- outputs: bfloat16 [64, 512, 768], P(('dp', 'ffn'))
- grad_inputs: float32 [64, 512, 768], P(('dp', 'ffn'))
- grad_w_qkv: float32 [768, 2304], P('dp', 'ffn')
- grad_w_out: float32 [768, 768], P('dp', 'ffn')
- grad_w_up: float32 [768, 3072], P('dp', 'ffn')
- grad_b_up: float32 [3072], P('ffn')
- grad_w_down: float32 [3072, 768], P('ffn', 'dp')
- grad_gains: float32 [2, 768], P(None, 'dp')
- grad_shifts: float32 [6, 768], P(None, 'dp')
- grad_logits: float32 [512, 512], P('dp', 'ffn')
Inputs may be any that keep to these rules, and one draw needn't show every extreme that they name: `token_counts_each`: number of real tokens of a sequence; the other positions of its 512 are padding, and only key positions are masked; some sequence has exactly 512 and some exactly 64.
All inputs are finite; a program needn't handle non-finite values.
Results may differ from a plain program's by a relative error of at most 0.012.
The roundings to bfloat16 on the way count: a program that leaves them out, or rounds other values in their place, can miss the bound.
Values may be sent and summed in bfloat16 or wider, within the bound.
A program may use at most 192 MiB of HBM per device.

v0:
```python
import jax
import jax.numpy as jnp
from jax import lax
from jax.sharding import PartitionSpec as P

D = 768
HEADS = 12
HEAD_DIM = 64
SEQ_LEN = 512
MICRO = 2


norm_eps = 1e-06


def split_up(value, dim, size):
    dims = value.shape
    parts = value.reshape(*dims[:dim], size, dims[dim] // size, *dims[dim + 1 :])
    return jnp.moveaxis(parts, dim, 0)


def summed_on_arrival(value, axis, dim):
    parts = split_up(value, dim, lax.axis_size(axis))
    arrived = lax.all_to_all(parts, axis, split_axis=0, concat_axis=0, tiled=True)
    return arrived.astype(jnp.float32).sum(axis=0)


def assemble(tile_stack, rows_dp, cols_ffn):
    count_all, first_len, second_len = tile_stack.shape
    grid = tile_stack.reshape(rows_dp, cols_ffn, first_len, second_len)
    return grid.transpose(0, 2, 1, 3).reshape(rows_dp * first_len, cols_ffn * second_len)


def disperse(full_grad, rows_dp, cols_ffn):
    total_rows, total_cols = full_grad.shape
    grid = full_grad.reshape(rows_dp, total_rows // rows_dp, cols_ffn, total_cols // cols_ffn)
    return grid.transpose(0, 2, 1, 3).reshape(
        rows_dp * cols_ffn, total_rows // rows_dp, total_cols // cols_ffn
    )


def vector_join(tile_stack, rows_dp, cols_ffn):
    count_all, kinds_count, part_len = tile_stack.shape
    picked = tile_stack.reshape(rows_dp, cols_ffn, kinds_count, part_len)[:, 0]
    return picked.transpose(1, 0, 2).reshape(kinds_count, rows_dp * part_len)


def vector_split(full_grad, rows_dp, cols_ffn):
    kinds_count, width_all = full_grad.shape
    part_len = width_all // rows_dp
    pieces = full_grad.reshape(kinds_count, rows_dp, part_len).transpose(1, 0, 2)
    spread = jnp.broadcast_to(pieces[:, None], (rows_dp, cols_ffn, kinds_count, part_len))
    return spread.reshape(rows_dp * cols_ffn, kinds_count, part_len)


def dot_first(left, right):
    return lax.dot_general(
        left, right, (((0,), (0,)), ((), ())), preferred_element_type=jnp.float32
    )


def dot_last(left, right):
    return lax.dot_general(
        left, right, (((1,), (1,)), ((), ())), preferred_element_type=jnp.float32
    )


def layer_norm(values, gain, shift):
    mean_row = jnp.mean(values, axis=-1, keepdims=True)
    centered = values - mean_row
    inv_std = lax.rsqrt(jnp.mean(centered * centered, axis=-1, keepdims=True) + norm_eps)
    normed = centered * inv_std
    return (normed * gain + shift, normed, inv_std)


def norm_back(grad_out, normed, inv_std, gain):
    grad_normed = grad_out * gain
    grad_in = inv_std * (
        grad_normed
        - jnp.mean(grad_normed, axis=-1, keepdims=True)
        - normed * jnp.mean(grad_normed * normed, axis=-1, keepdims=True)
    )
    return (grad_in, jnp.sum(grad_out * normed, axis=0), jnp.sum(grad_out, axis=0))


def gelu_slope(values):
    return (
        0.5 * (1.0 + lax.erf(values * 0.7071067811865476))
        + values * jnp.exp(-0.5 * values * values) * 0.3989422804014327
    )


def score_block(queries, keys_low, natural_log_gate, live):
    scores = (
        jnp.einsum("sqhd,skhd->shqk", queries, keys_low, preferred_element_type=jnp.float32)
        * HEAD_DIM ** (-0.5)
        + natural_log_gate
    )
    return jnp.where(live[:, None, None, :], scores, -1e30)


def attend(queries, keys_low, values_low, natural_log_gate, live):
    scores = score_block(queries, keys_low, natural_log_gate, live)
    peak = jnp.max(scores, axis=-1, keepdims=True)
    shifted_exp = jnp.exp(scores - peak)
    total_exp = jnp.sum(shifted_exp, axis=-1, keepdims=True)
    probs_low = (shifted_exp / total_exp).astype(jnp.bfloat16)
    context = jnp.einsum(
        "shqk,skhd->sqhd", probs_low, values_low, preferred_element_type=jnp.float32
    )
    return (context, peak + jnp.log(total_exp))


def attend_back(queries, keys_low, values_low, natural_log_gate, live, log_total, grad_context):
    scores = score_block(queries, keys_low, natural_log_gate, live)
    probs = jnp.exp(scores - log_total)
    grad_probs = jnp.einsum(
        "sqhd,skhd->shqk", grad_context, values_low, preferred_element_type=jnp.float32
    )
    grad_values = jnp.einsum(
        "shqk,sqhd->skhd",
        probs.astype(jnp.bfloat16),
        grad_context,
        preferred_element_type=jnp.float32,
    )
    grad_scores = probs * (grad_probs - jnp.sum(probs * grad_probs, axis=-1, keepdims=True))
    grad_mask = jnp.sum(grad_scores, axis=(0, 1))
    grad_scores_low = grad_scores.astype(jnp.bfloat16)
    grad_queries = jnp.einsum(
        "shqk,skhd->sqhd", grad_scores_low, keys_low, preferred_element_type=jnp.float32
    ) * HEAD_DIM ** (-0.5)
    grad_keys = jnp.einsum(
        "shqk,sqhd->skhd", grad_scores_low, queries, preferred_element_type=jnp.float32
    ) * HEAD_DIM ** (-0.5)
    return (grad_queries, grad_keys, grad_values, grad_mask)


def fetch_weights(
    attention_triple_matrix,
    attention_final_matrix,
    feedfwd_expand_matrix,
    feedfwd_contract_matrix,
    layernorm_scales,
    offset_vectors,
    learned_gate_scores,
    fixed_jitter_matrix,
    relaxation_heat,
):
    rows_dp = lax.axis_size("dp")
    cols_ffn = lax.axis_size("ffn")
    tiles = (
        lax.all_gather(attention_triple_matrix[None], ("dp", "ffn"), axis=0, tiled=True),
        lax.all_gather(attention_final_matrix[None], ("dp", "ffn"), axis=0, tiled=True),
        lax.all_gather(learned_gate_scores[None], ("dp", "ffn"), axis=0, tiled=True),
        lax.all_gather(fixed_jitter_matrix[None], ("dp", "ffn"), axis=0, tiled=True),
        lax.all_gather(layernorm_scales[None], ("dp", "ffn"), axis=0, tiled=True),
        lax.all_gather(offset_vectors[None], ("dp", "ffn"), axis=0, tiled=True),
    )
    ffn_parts = (
        lax.all_gather(feedfwd_expand_matrix, "dp", axis=0, tiled=True),
        lax.all_gather(feedfwd_contract_matrix, "dp", axis=1, tiled=True),
    )
    combined_attention_scores = (
        assemble(tiles[2], rows_dp, cols_ffn).astype(jnp.float32)
        + assemble(tiles[3], rows_dp, cols_ffn).astype(jnp.float32)
    ) / relaxation_heat[0]
    natural_log_gate = jax.nn.log_sigmoid(combined_attention_scores)
    gate_sharpness = jax.nn.sigmoid(-combined_attention_scores) / relaxation_heat[0]
    return (
        assemble(tiles[0], rows_dp, cols_ffn),
        assemble(tiles[1], rows_dp, cols_ffn),
        natural_log_gate,
        gate_sharpness,
        vector_join(tiles[4], rows_dp, cols_ffn).astype(jnp.float32),
        vector_join(tiles[5], rows_dp, cols_ffn).astype(jnp.float32),
        ffn_parts[0],
        ffn_parts[1],
    )


def reduce_grads(local_grads):
    rows_dp = lax.axis_size("dp")
    cols_ffn = lax.axis_size("ffn")
    grad_qkv, grad_out, grad_logit, grad_gain, grad_shift, grad_up, grad_down, grad_bias_up = (
        local_grads
    )
    attn_parts = (
        lax.psum_scatter(
            disperse(grad_qkv, rows_dp, cols_ffn), ("dp", "ffn"), scatter_dimension=0, tiled=True
        ),
        lax.psum_scatter(
            disperse(grad_out, rows_dp, cols_ffn), ("dp", "ffn"), scatter_dimension=0, tiled=True
        ),
        lax.psum_scatter(
            disperse(grad_logit, rows_dp, cols_ffn), ("dp", "ffn"), scatter_dimension=0, tiled=True
        ),
        lax.psum_scatter(
            vector_split(grad_gain, rows_dp, cols_ffn),
            ("dp", "ffn"),
            scatter_dimension=0,
            tiled=True,
        ),
        lax.psum_scatter(
            vector_split(grad_shift, rows_dp, cols_ffn),
            ("dp", "ffn"),
            scatter_dimension=0,
            tiled=True,
        ),
    )
    bias_rows = jnp.broadcast_to(grad_bias_up[None], (rows_dp, grad_bias_up.shape[0]))
    ffn_parts = (
        summed_on_arrival(grad_up.astype(jnp.bfloat16), "dp", 0),
        summed_on_arrival(grad_down.astype(jnp.bfloat16), "dp", 1),
        summed_on_arrival(bias_rows.astype(jnp.bfloat16), "dp", 0),
    )
    return (
        attn_parts[0][0],
        attn_parts[1][0],
        attn_parts[2][0],
        attn_parts[3][0],
        attn_parts[4][0],
        ffn_parts[0],
        ffn_parts[1],
        ffn_parts[2][0],
    )


def micro_step(fetched, inputs_block, lengths_block, cot_block, feedfwd_expand_offset):
    (
        full_qkv,
        full_out,
        natural_log_gate,
        gate_sharpness,
        gains_full,
        shifts_full,
        full_up,
        full_down,
    ) = fetched
    seq_count = inputs_block.shape[0]
    row_count = seq_count * SEQ_LEN
    flat_in = inputs_block.reshape(row_count, D)
    qkv_bias = jnp.concatenate([shifts_full[0], jnp.zeros((D,), jnp.float32), shifts_full[1]])
    proj_low = (jnp.dot(flat_in, full_qkv, preferred_element_type=jnp.float32) + qkv_bias).astype(
        jnp.bfloat16
    )
    head_shape = (seq_count, SEQ_LEN, HEADS, HEAD_DIM)
    queries = proj_low[:, :D].reshape(head_shape)
    keys_low = proj_low[:, D : 2 * D].reshape(head_shape)
    values_low = proj_low[:, 2 * D :].reshape(head_shape)
    live = lax.broadcasted_iota(jnp.int32, (seq_count, SEQ_LEN), 1) < lengths_block[:, None]
    context, log_total = attend(queries, keys_low, values_low, natural_log_gate, live)
    context_low = context.reshape(row_count, D).astype(jnp.bfloat16)
    first_sum = (
        flat_in.astype(jnp.float32)
        + jnp.dot(context_low, full_out, preferred_element_type=jnp.float32)
        + shifts_full[2]
    )
    hidden, normed_one, inv_one = layer_norm(first_sum, gains_full[0], shifts_full[4])
    hidden_low = hidden.astype(jnp.bfloat16)
    gathered = lax.all_gather(hidden_low, "ffn", axis=0, tiled=True)
    pre_act = jnp.dot(
        gathered, full_up, preferred_element_type=jnp.float32
    ) + feedfwd_expand_offset.astype(jnp.float32)
    act_low = jax.nn.gelu(pre_act, approximate=False).astype(jnp.bfloat16)
    partial_out = jnp.dot(act_low, full_down, preferred_element_type=jnp.float32)
    ffn_out = lax.psum_scatter(partial_out, "ffn", scatter_dimension=0, tiled=True)
    second_sum = hidden + ffn_out + shifts_full[3]
    result, normed_two, inv_two = layer_norm(second_sum, gains_full[1], shifts_full[5])
    cot_flat = cot_block.reshape(row_count, D).astype(jnp.float32)
    grad_second, grad_gain_two, grad_shift_two = norm_back(
        cot_flat, normed_two, inv_two, gains_full[1]
    )
    grad_second_low = grad_second.astype(jnp.bfloat16)
    grad_gathered = lax.all_gather(grad_second_low, "ffn", axis=0, tiled=True)
    grad_w_down = dot_first(act_low, grad_gathered)
    grad_act = dot_last(grad_gathered, full_down)
    grad_pre = (grad_act * gelu_slope(pre_act)).astype(jnp.bfloat16)
    grad_bias_up = jnp.sum(grad_pre, axis=0, dtype=jnp.float32)
    grad_w_up = dot_first(gathered, grad_pre)
    grad_hidden_part = dot_last(grad_pre, full_up)
    grad_hidden_ffn = lax.psum_scatter(grad_hidden_part, "ffn", scatter_dimension=0, tiled=True)
    grad_hidden = grad_second + grad_hidden_ffn
    grad_first, grad_gain_one, grad_shift_one = norm_back(
        grad_hidden, normed_one, inv_one, gains_full[0]
    )
    grad_first_low = grad_first.astype(jnp.bfloat16)
    grad_w_out = dot_first(context_low, grad_first_low)
    grad_context = dot_last(grad_first_low, full_out).astype(jnp.bfloat16).reshape(head_shape)
    grad_queries, grad_keys, grad_values, grad_mask = attend_back(
        queries, keys_low, values_low, natural_log_gate, live, log_total, grad_context
    )
    grad_projected = jnp.concatenate(
        [
            grad_queries.reshape(row_count, D).astype(jnp.bfloat16),
            grad_keys.reshape(row_count, D).astype(jnp.bfloat16),
            grad_values.reshape(row_count, D).astype(jnp.bfloat16),
        ],
        axis=1,
    )
    grad_w_qkv = dot_first(flat_in, grad_projected)
    grad_inputs = grad_first + dot_last(grad_projected, full_qkv)
    grad_query_bias = jnp.sum(grad_projected[:, :D], axis=0, dtype=jnp.float32)
    grad_value_bias = jnp.sum(grad_projected[:, 2 * D :], axis=0, dtype=jnp.float32)
    grad_shift_all = jnp.stack(
        [
            grad_query_bias,
            grad_value_bias,
            jnp.sum(grad_first, axis=0),
            jnp.sum(grad_second, axis=0),
            grad_shift_one,
            grad_shift_two,
        ]
    )
    grad_gain_all = jnp.stack([grad_gain_one, grad_gain_two])
    grad_logit = grad_mask * gate_sharpness
    local_grads = (
        grad_w_qkv,
        grad_w_out,
        grad_logit,
        grad_gain_all,
        grad_shift_all,
        grad_w_up,
        grad_w_down,
        grad_bias_up,
    )
    return (
        result.astype(jnp.bfloat16).reshape(seq_count, SEQ_LEN, D),
        grad_inputs.reshape(seq_count, SEQ_LEN, D),
        local_grads,
    )


def on_device(
    layer_activations,
    token_counts_each,
    attention_triple_matrix,
    attention_final_matrix,
    feedfwd_expand_matrix,
    feedfwd_expand_offset,
    feedfwd_contract_matrix,
    layernorm_scales,
    offset_vectors,
    learned_gate_scores,
    fixed_jitter_matrix,
    relaxation_heat,
    loss_grad_result,
):
    seq_block = layer_activations.shape[0] // MICRO
    result_list = []
    grad_list = []
    summed = None
    for micro_index in range(MICRO):
        fetched = fetch_weights(
            attention_triple_matrix,
            attention_final_matrix,
            feedfwd_expand_matrix,
            feedfwd_contract_matrix,
            layernorm_scales,
            offset_vectors,
            learned_gate_scores,
            fixed_jitter_matrix,
            relaxation_heat,
        )
        begin = micro_index * seq_block
        result_block, grad_block, local_grads = micro_step(
            fetched,
            layer_activations[begin : begin + seq_block],
            token_counts_each[begin : begin + seq_block],
            loss_grad_result[begin : begin + seq_block],
            feedfwd_expand_offset,
        )
        result_list.append(result_block)
        grad_list.append(grad_block)
        reduced = reduce_grads(local_grads)
        if summed is None:
            summed = reduced
        else:
            summed = tuple((left + right for left, right in zip(summed, reduced)))
    return (
        jnp.concatenate(result_list, axis=0),
        jnp.concatenate(grad_list, axis=0),
        summed[0],
        summed[1],
        summed[5],
        summed[7],
        summed[6],
        summed[3],
        summed[4],
        summed[2],
    )


def solution(mesh):
    in_specs = (
        P(("dp", "ffn"), None, None),
        P(("dp", "ffn")),
        P("dp", "ffn"),
        P("dp", "ffn"),
        P("dp", "ffn"),
        P("ffn"),
        P("ffn", "dp"),
        P(None, "dp"),
        P(None, "dp"),
        P("dp", "ffn"),
        P("dp", "ffn"),
        P(),
        P(("dp", "ffn"), None, None),
    )
    out_specs = (
        P(("dp", "ffn"), None, None),
        P(("dp", "ffn"), None, None),
        P("dp", "ffn"),
        P("dp", "ffn"),
        P("dp", "ffn"),
        P("ffn"),
        P("ffn", "dp"),
        P(None, "dp"),
        P(None, "dp"),
        P("dp", "ffn"),
    )
    return jax.shard_map(
        on_device, mesh=mesh, in_specs=in_specs, out_specs=out_specs, check_vma=False
    )
```

profile of v0, /device:TPU:0, one launch (start us, length us, event | category | flops | bytes accessed | tf_op | source)
XLA Modules:
  0.0 1699.8 jit_solution(4556506373768897747)
XLA Ops:
  13.2 69.5 %all-gather.7 = bf16[32,2,96]{2,1,0:T(2,128)(2,1)S(1)} all-gather(bf16[1,2,96]{2,1,0:T(2,128)(2,1)} %bitcast.336), channel_id=7, replica_groups=mesh['dp'=8,'ffn'=4] {'dp','ffn'}, dimensions={0}, use_global_device_ids=true | all-gather | bytes 12672 | tf_op jit(solution)/shard_map/all_gather | solution.py:156
  82.7 64.6 %all-gather.6 = bf16[32,6,96]{2,1,0:T(8,128)(2,1)S(1)} all-gather(bf16[1,6,96]{2,1,0:T(8,128)(2,1)} %bitcast.335), channel_id=3, replica_groups=mesh['dp'=8,'ffn'=4] {'dp','ffn'}, dimensions={0}, use_global_device_ids=true | all-gather | bytes 38016 | tf_op jit(solution)/shard_map/all_gather | solution.py:157
  148.4 70.6 %all-gather.2 = bf16[2048,128]{1,0:T(8,128)(2,1)S(1)} all-gather(bf16[64,128]{1,0:T(8,128)(2,1)} %param.22), channel_id=4, replica_groups=mesh['dp'=8,'ffn'=4] {'dp','ffn'}, dimensions={0}, use_global_device_ids=true | all-gather | bytes 540672 | tf_op jit(solution)/shard_map/all_gather | solution.py:154
  219.0 68.3 %all-gather.3 = bf16[2048,128]{1,0:T(8,128)(2,1)S(1)} all-gather(bf16[64,128]{1,0:T(8,128)(2,1)} %param.23), channel_id=5, replica_groups=mesh['dp'=8,'ffn'=4] {'dp','ffn'}, dimensions={0}, use_global_device_ids=true | all-gather | bytes 540672 | tf_op jit(solution)/shard_map/all_gather | solution.py:155
  296.0 6.0 copy.232
  302.0 6.7 reshape.581
  308.7 3.8 fusion.45
  312.6 3.4 fusion.44
  317.9 3.2 fusion.110
  325.2 4.8 fusion.113
  334.7 3.6 fusion.75
  338.4 3.8 fusion.115
  355.1 59.9 %all-gather.23.cloned.1.call-done = bf16[2048,768]{1,0:T(8,128)(2,1)} async-done(((bf16[512,768]{1,0:T(8,128)(2,1)}), bf16[2048,768]{1,0:T(8,128)(2,1)}) %all-gather.23.cloned.1.call-update) | async-done | bytes 3145744 | tf_op jit(solution)/shard_map/all_gather | solution.py:260
  415.0 7.6 fusion.120
  422.5 56.6 %all-gather.17.cloned.1.call-done = bf16[2048,768]{1,0:T(8,128)(2,1)} async-done(((bf16[512,768]{1,0:T(8,128)(2,1)}), bf16[2048,768]{1,0:T(8,128)(2,1)}) %all-gather.17.cloned.1.call-update) | async-done | bytes 3145744 | tf_op jit(solution)/shard_map/all_gather | solution.py:260
  479.2 32.5 %fusion.6 = (bf16[2048,768]{1,0:T(8,128)(2,1)}, bf16[2048,768]{1,0:T(8,128)(2,1)}, f32[2048,768]{1,0:T(8,128)}) fusion(f32[768]{0:T(1024)S(1)} %convert_element_type.336, f32[2048,768]{1,0:T(8,128)} %fusion.120, bf16[2048,768]{1,0:T(8,128)(2,1)} %all-gather.17.cloned.1.call-done, bf16[768,768]{1,0:T(8,128)(2,1)} %all-gather.19.cloned.1.call-done), kind=kOutput, calls=%fused_computation.23 | convolution fusion | flops 2623537152 | bytes 23202816 | tf_op jit(solution)/shard_map/dot_general | solution.py:261
  511.7 7.5 fusion.119
  519.3 7.5 fusion.121
  527.7 101.1 %reduce-scatter.8.cloned.1.call-done = f32[512,768]{1,0:T(8,128)} async-done(((f32[2048,768]{1,0:T(8,128)}), f32[512,768]{1,0:T(8,128)}) %reduce-scatter.8.cloned.1.call-update) | async-done | bytes 1572880 | tf_op jit(solution)/shard_map/reduce_scatter | solution.py:266
  628.8 113.6 %reduce-scatter.10.cloned.1.call-done = f32[512,768]{1,0:T(8,128)} async-done(((f32[2048,768]{1,0:T(8,128)}), f32[512,768]{1,0:T(8,128)}) %reduce-scatter.10.cloned.1.call-update) | async-done | bytes 1572880 | tf_op jit(solution)/shard_map/reduce_scatter | solution.py:266
  742.4 2.9 fusion.108
  756.4 61.5 %all-gather.25.cloned.1.call-done = bf16[2048,768]{1,0:T(8,128)(2,1)} async-done(((bf16[512,768]{1,0:T(8,128)(2,1)}), bf16[2048,768]{1,0:T(8,128)(2,1)}) %all-gather.25.cloned.1.call-update) | async-done | bytes 3145744 | tf_op jit(solution)/shard_map/all_gather | solution.py:274
  817.9 7.4 fusion.117
  827.0 4.6 fusion.122
  831.6 49.8 %all-gather.27.cloned.1.call-done = bf16[2048,768]{1,0:T(8,128)(2,1)} async-done(((bf16[512,768]{1,0:T(8,128)(2,1)}), bf16[2048,768]{1,0:T(8,128)(2,1)}) %all-gather.27.cloned.1.call-update) | async-done | bytes 3145744 | tf_op jit(solution)/shard_map/all_gather | solution.py:274
  881.5 7.4 fusion.118
  890.7 4.6 fusion.123
  897.4 95.8 %reduce-scatter.12.cloned.1.call-done = f32[512,768]{1,0:T(8,128)} async-done(((f32[2048,768]{1,0:T(8,128)}), f32[512,768]{1,0:T(8,128)}) %reduce-scatter.12.cloned.1.call-update) | async-done | bytes 1572880 | tf_op jit(solution)/shard_map/reduce_scatter | solution.py:281
  993.2 3.7 multiply_reduce_fusion.3
  997.0 109.7 %reduce-scatter.14.cloned.1.call-done = f32[512,768]{1,0:T(8,128)} async-done(((f32[2048,768]{1,0:T(8,128)}), f32[512,768]{1,0:T(8,128)}) %reduce-scatter.14.cloned.1.call-update) | async-done | bytes 1572880 | tf_op jit(solution)/shard_map/reduce_scatter | solution.py:281
  1106.7 4.2 fusion.107
  1113.1 7.6 convert_reduce_fusion.8
  1120.7 8.9 multiply_reduce_fusion.1
  1132.0 7.6 convert_reduce_fusion.6
  1139.6 8.8 multiply_reduce_fusion
  1148.9 13.7 fusion.46
  1167.8 4.8 convert_reduce_fusion.9
  1172.6 13.6 fusion.48
  1191.4 3.9 convert_reduce_fusion.7
  1211.4 5.0 multiply_convert_fusion.2
  1221.4 5.1 add_bitcast_fusion
  1226.5 8.0 copy.206
  1234.5 10.4 reshape.651
  1244.9 7.3 copy.207
  1254.1 3.6 all-to-all-start.3
  1259.1 3.4 all-to-all-done.3
  1262.4 3.3 all-to-all-start.2
  1265.8 6.6 convolution_convert_fusion
  1272.4 4.5 all-to-all-start.5
  1277.0 6.5 convolution_convert_fusion.2
  1283.5 10.3 all-to-all-done.5
  1293.8 4.3 all-to-all-start.1
  1298.1 6.6 convolution_convert_fusion.1
  1304.7 10.5 all-to-all-done.1
  1315.2 4.3 all-to-all-start.4
  1319.5 6.6 convolution_convert_fusion.3
  1326.1 10.4 all-to-all-done.4
  1336.4 4.3 all-to-all-start
  1349.2 8.9 all-to-all-done
  1360.5 39.7 %all-reduce = f32[32,2,96]{2,1,0:T(2,128)S(1)} all-reduce(f32[32,2,96]{2,1,0:T(2,128)S(1)} %bitcast.332), channel_id=19, replica_groups=mesh['dp'=8,'ffn'=4] {'dp','ffn'}, use_global_device_ids=true, to_apply=%region_40.41.clone | all-reduce | flops 6144 | bytes 49152
  1400.8 5.2 add_bitcast_fusion.2
  1411.2 48.5 %reduce-scatter.20.cloned.1.call-done = f32[1,64,128]{2,1,0:T(8,128)} async-done(((f32[32,64,128]{2,1,0:T(8,128)}), f32[1,64,128]{2,1,0:T(8,128)}) %reduce-scatter.20.cloned.1.call-update) | async-done | bytes 32784 | tf_op jit(solution)/shard_map/reduce_scatter | solution.py:194
  1459.7 104.6 %reduce-scatter.18.cloned.1.call-done = f32[1,96,192]{2,1,0:T(8,128)} async-done(((f32[32,96,192]{2,1,0:T(8,128)}), f32[1,96,192]{2,1,0:T(8,128)}) %reduce-scatter.18.cloned.1.call-update) | async-done | bytes 73744 | tf_op jit(solution)/shard_map/reduce_scatter | solution.py:191
  1564.2 128.5 %reduce-scatter.16.cloned.1.call-done = f32[1,96,576]{2,1,0:T(8,128)} async-done(((f32[32,96,576]{2,1,0:T(8,128)}), f32[1,96,576]{2,1,0:T(8,128)}) %reduce-scatter.16.cloned.1.call-update) | async-done | bytes 221200 | tf_op jit(solution)/shard_map/reduce_scatter | solution.py:188
  (288 shorter events, 112.0 us)
Async XLA Ops:
  7.2 284.6 %all-gather.31.cloned.1.call-start = ((), (), s32[]{:S(2)}) async-start(), calls=%async_computation.24 | async-start | bytes 1622016 | tf_op jit(solution)/shard_map/all_gather | solution.py:153
  7.9 288.0 %all-gather.29.cloned.1.call-start = ((), (), s32[]{:S(2)}) async-start(), calls=%async_computation.23 | async-start | bytes 4055040 | tf_op jit(solution)/shard_map/all_gather | solution.py:152
  8.7 346.4 %all-gather.19.cloned.1.call-start = ((), (), s32[]{:S(2)}) async-start(), calls=%async_computation.14 | async-start | bytes 1327104 | tf_op jit(solution)/shard_map/all_gather | solution.py:160
  9.4 405.6 %all-gather.23.cloned.1.call-start = ((), (), s32[]{:S(2)}) async-start(), calls=%async_computation.17 | async-start | bytes 3932160 | tf_op jit(solution)/shard_map/all_gather | solution.py:260
  308.7 3.9 copy-start.10
  308.7 3.9 copy-start.36
  308.7 3.9 copy-start.52
  316.5 21.9 %copy-start.4 = (bf16[512,768]{0,1:T(8,128)(2,1)}, bf16[512,768]{0,1:T(8,128)(2,1)S(1)}, u32[]{:S(2)}) copy-start(bf16[512,768]{0,1:T(8,128)(2,1)S(1)} %copy.196) | copy-start | bytes 2359300
  317.9 26.2 %copy-start.12 = (bf16[512,768]{0,1:T(8,128)(2,1)}, bf16[512,768]{0,1:T(8,128)(2,1)S(1)}, u32[]{:S(2)}) copy-start(bf16[512,768]{0,1:T(8,128)(2,1)S(1)} %copy.194) | copy-start | bytes 2359300
  321.1 4.0 copy-start.56
  322.6 7.4 copy-start.6
  325.2 6.7 copy-start.14
  330.0 4.5 copy-start.1
  330.0 4.7 copy-start.39
  331.8 6.6 copy-start.41
  334.7 3.7 copy-start.19
  334.7 3.7 copy-start.30
  342.3 4.6 copy-start
  342.3 4.7 copy-start.43
  344.1 5.4 copy-start.45
  347.0 2.5 copy-start.27
  347.0 2.5 copy-start.31
  347.0 2.5 copy-start.37
  352.1 2.9 copy-start.53
  353.8 125.4 %all-gather.17.cloned.1.call-start = ((), (), s32[]{:S(2)}) async-start(), calls=%async_computation.13 | async-start | bytes 3932160 | tf_op jit(solution)/shard_map/all_gather | solution.py:260
  354.4 157.3 %all-gather.21.cloned.1.call-start = ((), (), s32[]{:S(2)}) async-start(), calls=%async_computation.15 | async-start | bytes 1327104 | tf_op jit(solution)/shard_map/all_gather | solution.py:161
  355.0 273.8 %reduce-scatter.8.cloned.1.call-start = ((), (), s32[]{:S(2)}) async-start(), calls=%async_computation.16 | async-start | bytes 7864320 | tf_op jit(solution)/shard_map/reduce_scatter | solution.py:266
  519.2 223.2 %reduce-scatter.10.cloned.1.call-start = ((), (), s32[]{:S(2)}) async-start(), calls=%async_computation.18 | async-start | bytes 7864320 | tf_op jit(solution)/shard_map/reduce_scatter | solution.py:266
  526.8 291.1 %all-gather.25.cloned.1.call-start = ((), (), s32[]{:S(2)}) async-start(), calls=%async_computation.19 | async-start | bytes 3932160 | tf_op jit(solution)/shard_map/all_gather | solution.py:274
  753.7 127.8 %all-gather.27.cloned.1.call-start = ((), (), s32[]{:S(2)}) async-start(), calls=%async_computation.21 | async-start | bytes 3932160 | tf_op jit(solution)/shard_map/all_gather | solution.py:274
  756.3 236.9 %reduce-scatter.12.cloned.1.call-start = ((), (), s32[]{:S(2)}) async-start(), calls=%async_computation.20 | async-start | bytes 7864320 | tf_op jit(solution)/shard_map/reduce_scatter | solution.py:281
  817.9 9.1 copy-start.54
  831.6 275.1 %reduce-scatter.14.cloned.1.call-start = ((), (), s32[]{:S(2)}) async-start(), calls=%async_computation.22 | async-start | bytes 7864320 | tf_op jit(solution)/shard_map/reduce_scatter | solution.py:281
  881.5 9.2 copy-start.55
  895.3 514.6 %all-reduce.4.cloned.1.call-start = ((), (), s32[]{:S(2)}) async-start(), calls=%async_computation.28 | async-start | bytes 262144
  1106.7 5.3 copy-start.28
  1113.1 7.6 copy-start.15
  1120.7 8.9 copy-start.9
  1132.0 7.6 copy-start.13
  1162.6 5.2 copy-start.7
  1186.2 5.2 copy-start.5
  1196.2 263.5 %reduce-scatter.20.cloned.1.call-start = ((), (), s32[]{:S(2)}) async-start(), calls=%async_computation.27 | async-start | bytes 1081344 | tf_op jit(solution)/shard_map/reduce_scatter | solution.py:194
  1200.2 364.0 %reduce-scatter.18.cloned.1.call-start = ((), (), s32[]{:S(2)}) async-start(), calls=%async_computation.26 | async-start | bytes 3244032 | tf_op jit(solution)/shard_map/reduce_scatter | solution.py:191
  1205.3 2.3 copy-start.22
  1205.3 2.3 copy-start.34
  1210.3 482.4 %reduce-scatter.16.cloned.1.call-start = ((), (), s32[]{:S(2)}) async-start(), calls=%async_computation.25 | async-start | bytes 8110080 | tf_op jit(solution)/shard_map/reduce_scatter | solution.py:188
  1211.4 5.0 copy-start.25
  1211.4 5.0 copy-start.32
  1211.4 5.0 copy-start.38
  1211.4 7.0 slice-start
  1218.5 2.9 copy-start.17
  1254.1 8.4 all-to-all-start.3
  1262.4 10.0 all-to-all-start.2
  1272.4 21.4 %all-to-all-start.5 = ((bf16[8,768,96]{1,2,0:T(8,128)(2,1)}), bf16[8,768,96]{1,2,0:T(8,128)(2,1)}, u32[]{:S(2)}, u32[]{:S(2)}) async-start(bf16[8,768,96]{1,2,0:T(8,128)(2,1)} %bitcast.320), calls=%async_computation.9 | async-start | bytes 2359296 | tf_op jit(solution)/shard_map/all_to_all | solution.py:24
  1293.8 21.3 %all-to-all-start.1 = ((bf16[8,96,768]{2,1,0:T(8,128)(2,1)}), bf16[8,96,768]{2,1,0:T(8,128)(2,1)}, u32[]{:S(2)}, u32[]{:S(2)}) async-start(bf16[8,96,768]{2,1,0:T(8,128)(2,1)} %bitcast.321), calls=%async_computation.5 | async-start | bytes 2359296 | tf_op jit(solution)/shard_map/all_to_all | solution.py:24
  1315.2 21.3 %all-to-all-start.4 = ((bf16[8,768,96]{1,2,0:T(8,128)(2,1)}), bf16[8,768,96]{1,2,0:T(8,128)(2,1)}, u32[]{:S(2)}, u32[]{:S(2)}) async-start(bf16[8,768,96]{1,2,0:T(8,128)(2,1)} %bitcast.322), calls=%async_computation.8 | async-start | bytes 2359296 | tf_op jit(solution)/shard_map/all_to_all | solution.py:24
  1319.4 21.3 %copy-start.51 = (f32[768]{0:T(1024)S(1)}, f32[768]{0:T(1024)}, u32[]{:S(2)}) copy-start(f32[768]{0:T(1024)} %get-tuple-element.16) | copy-start | bytes 9220
  1319.4 21.3 %copy-start.50 = (f32[768]{0:T(1024)S(1)}, f32[768]{0:T(1024)}, u32[]{:S(2)}) copy-start(f32[768]{0:T(1024)} %get-tuple-element.19) | copy-start | bytes 9220
  1319.5 21.4 %copy-start.16 = (bf16[1,512,768]{2,1,0:T(8,128)(2,1)S(1)}, bf16[1,512,768]{2,1,0:T(8,128)(2,1)}, u32[]{:S(2)}) copy-start(bf16[1,512,768]{2,1,0:T(8,128)(2,1)} %get-tuple-element.61) | copy-start | bytes 2359300
  1336.4 21.6 %all-to-all-start = ((bf16[8,96,768]{2,1,0:T(8,128)(2,1)}), bf16[8,96,768]{2,1,0:T(8,128)(2,1)}, u32[]{:S(2)}, u32[]{:S(2)}) async-start(bf16[8,96,768]{2,1,0:T(8,128)(2,1)} %bitcast.319), calls=%async_computation.4 | async-start | bytes 2359296 | tf_op jit(solution)/shard_map/all_to_all | solution.py:24
  1345.4 55.3 %copy-start.26 = (bf16[12,64,512]{2,1,0:T(8,128)(2,1)S(1)}, bf16[12,64,512]{2,1,0:T(8,128)(2,1)}, u32[]{:S(2)}) copy-start(bf16[12,64,512]{2,1,0:T(8,128)(2,1)} %get-tuple-element.98) | copy-start | bytes 2359300
  1400.8 5.2 copy-start.11
  1400.8 5.2 copy-start.18
  1400.8 5.2 copy-start.24
  (19 other events, 27.7 us)
Sparse Core Ops, SparseCore 0:
  10.9 57.7 all-gather.30
  71.5 60.2 all-gather.28
  133.7 22.7 all-gather.18
  353.9 61.0 all-gather.22
  417.0 62.1 all-gather.16
  480.9 22.7 all-gather.20
  519.4 109.3 reduce-scatter.7
  631.1 111.2 reduce-scatter.9
  753.8 64.0 all-gather.24
  819.3 62.1 all-gather.26
  883.8 109.3 reduce-scatter.11
  995.4 111.2 reduce-scatter.13
  1196.3 124.6 all-reduce.3
  1323.7 135.9 reduce-scatter.19
  1466.4 97.8 reduce-scatter.17
  1571.3 121.4 reduce-scatter.15
where the time goes:
time: 1710 us; the launch traced here: 1700 us
  waiting for transfers between devices  976 us (57%)
  blocking collectives  313 us (18%)
  matrix products  199 us (12%)
  local copies, waits for them, and re-layouts  92 us (5%)
  other arithmetic  78.4 us (5%)
  starting transfers between devices  25.4 us (1%)
    reduce_scatter x2, waiting for transfers between devices, micro_step(): lax.psum_scatter(partial_out, 'ffn', scatter_dimension=0, tiled=True)  215 us
    reduce_scatter x2, waiting for transfers between devices, micro_step(): lax.psum_scatter(grad_hidden_part, 'ffn', scatter_dimension=0, tiled=True)  206 us
    reduce_scatter x1, waiting for transfers between devices, reduce_grads(): lax.psum_scatter(disperse(grad_qkv, rows_dp, cols_ffn), ('dp', 'ffn'), sc...  129 us
    all_gather x2, waiting for transfers between devices, micro_step(): gathered = lax.all_gather(hidden_low, 'ffn', axis=0, tiled=True)  117 us
    all_gather x2, waiting for transfers between devices, micro_step(): grad_gathered = lax.all_gather(grad_second_low, 'ffn', axis=0, tiled=True)  111 us
    reduce_scatter x1, waiting for transfers between devices, reduce_grads(): lax.psum_scatter(disperse(grad_out, rows_dp, cols_ffn), ('dp', 'ffn'), sc...  105 us
    all_gather x1, blocking collectives, fetch_weights(): lax.all_gather(learned_gate_scores[None], ('dp', 'ffn'), axis=0, tiled=True)  70.6 us
    all_gather x1, blocking collectives, fetch_weights(): lax.all_gather(layernorm_scales[None], ('dp', 'ffn'), axis=0, tiled=True)  69.5 us
  transfers between devices with their start and end apart: 22, of which 16 were waited for; matrix products, arithmetic and copies ran while one was open for 15% of the time, Pallas kernels for 0%

commit v1 on v0

v1 whole, which is shorter than its diff:
```python
import jax
import jax.numpy as jnp
from jax import lax
from jax.sharding import PartitionSpec as P

D = 768
HEADS = 12
HEAD_DIM = 64
SEQ_LEN = 512
AXES = ("dp", "ffn")
norm_eps = 1e-06
f32 = jnp.float32
bf16 = jnp.bfloat16


def dot_first(left, right):
    return lax.dot_general(left, right, (((0,), (0,)), ((), ())), preferred_element_type=f32)


def dot_last(left, right):
    return lax.dot_general(left, right, (((1,), (1,)), ((), ())), preferred_element_type=f32)


def dot(left, right):
    return jnp.dot(left, right, preferred_element_type=f32)


def layer_norm(values, gain, shift):
    mean_row = jnp.mean(values, axis=-1, keepdims=True)
    centered = values - mean_row
    inv_std = lax.rsqrt(jnp.mean(centered * centered, axis=-1, keepdims=True) + norm_eps)
    normed = centered * inv_std
    return (normed * gain + shift, normed, inv_std)


def norm_back(grad_out, normed, inv_std, gain):
    grad_normed = grad_out * gain
    grad_in = inv_std * (
        grad_normed
        - jnp.mean(grad_normed, axis=-1, keepdims=True)
        - normed * jnp.mean(grad_normed * normed, axis=-1, keepdims=True)
    )
    return (grad_in, jnp.sum(grad_out * normed, axis=0), jnp.sum(grad_out, axis=0))


def gelu_slope(values):
    return (
        0.5 * (1.0 + lax.erf(values * 0.7071067811865476))
        + values * jnp.exp(-0.5 * values * values) * 0.3989422804014327
    )


def score_block(queries, keys_low, natural_log_gate, live):
    scores = (
        jnp.einsum("qhd,khd->hqk", queries, keys_low, preferred_element_type=f32)
        * HEAD_DIM ** (-0.5)
        + natural_log_gate
    )
    return jnp.where(live[None, None, :], scores, -1e30)


def attend(queries, keys_low, values_low, natural_log_gate, live):
    scores = score_block(queries, keys_low, natural_log_gate, live)
    peak = jnp.max(scores, axis=-1, keepdims=True)
    shifted_exp = jnp.exp(scores - peak)
    total_exp = jnp.sum(shifted_exp, axis=-1, keepdims=True)
    probs_low = (shifted_exp / total_exp).astype(bf16)
    context = jnp.einsum("hqk,khd->qhd", probs_low, values_low, preferred_element_type=f32)
    return (context, peak + jnp.log(total_exp))


def attend_back(queries, keys_low, values_low, natural_log_gate, live, log_total, grad_context):
    scores = score_block(queries, keys_low, natural_log_gate, live)
    probs = jnp.exp(scores - log_total)
    grad_probs = jnp.einsum("qhd,khd->hqk", grad_context, values_low, preferred_element_type=f32)
    grad_values = jnp.einsum(
        "hqk,qhd->khd", probs.astype(bf16), grad_context, preferred_element_type=f32
    )
    grad_scores = probs * (grad_probs - jnp.sum(probs * grad_probs, axis=-1, keepdims=True))
    grad_mask = jnp.sum(grad_scores, axis=0)
    grad_scores_low = grad_scores.astype(bf16)
    grad_queries = jnp.einsum(
        "hqk,khd->qhd", grad_scores_low, keys_low, preferred_element_type=f32
    ) * HEAD_DIM ** (-0.5)
    grad_keys = jnp.einsum(
        "hqk,qhd->khd", grad_scores_low, queries, preferred_element_type=f32
    ) * HEAD_DIM ** (-0.5)
    return (grad_queries, grad_keys, grad_values, grad_mask)


def gather_weights(pack, small):
    rows_dp = lax.axis_size("dp")
    cols_ffn = lax.axis_size("ffn")
    full = lax.all_gather(pack[None], AXES, axis=0, tiled=True)
    full = full.reshape(rows_dp, cols_ffn, *pack.shape)
    small_full = lax.all_gather(small[None], AXES, axis=0, tiled=True)
    return full, small_full.reshape(rows_dp, cols_ffn, *small.shape)


def columns(blocks):
    rows_dp, cols_ffn, rows, cols = blocks.shape
    return blocks.transpose(0, 2, 1, 3).reshape(rows_dp * rows, cols_ffn * cols)


def blocks_of(full, rows_dp, cols_ffn):
    rows, cols = full.shape
    return full.reshape(rows_dp, rows // rows_dp, cols_ffn, cols // cols_ffn).transpose(0, 2, 1, 3)


def on_device(
    layer_activations,
    token_counts_each,
    attention_triple_matrix,
    attention_final_matrix,
    feedfwd_expand_matrix,
    feedfwd_expand_offset,
    feedfwd_contract_matrix,
    layernorm_scales,
    offset_vectors,
    learned_gate_scores,
    fixed_jitter_matrix,
    relaxation_heat,
    loss_grad_result,
):
    rows_dp = lax.axis_size("dp")
    cols_ffn = lax.axis_size("ffn")
    seq_count = layer_activations.shape[0]
    row_count = seq_count * SEQ_LEN
    shard_rows = attention_triple_matrix.shape[0]
    qkv_cols = attention_triple_matrix.shape[1]
    out_cols = attention_final_matrix.shape[1]
    ff_cols = feedfwd_expand_matrix.shape[1]

    pack = jnp.concatenate(
        [
            attention_triple_matrix,
            attention_final_matrix,
            feedfwd_expand_matrix,
            feedfwd_contract_matrix.T,
        ],
        axis=1,
    )
    mask_cols = learned_gate_scores.shape[1]
    vectors = jnp.concatenate([layernorm_scales, offset_vectors], axis=0)
    small = jnp.concatenate(
        [
            learned_gate_scores,
            fixed_jitter_matrix,
            jnp.pad(vectors, ((0, 0), (0, mask_cols - vectors.shape[1]))),
            feedfwd_expand_offset.reshape(-1, mask_cols),
        ],
        axis=0,
    )
    full, small_full = gather_weights(pack, small)
    full_qkv = columns(full[..., :qkv_cols])
    full_out = columns(full[..., qkv_cols : qkv_cols + out_cols])
    full_up = columns(full[..., qkv_cols + out_cols : qkv_cols + out_cols + ff_cols])
    full_down_t = columns(full[..., qkv_cols + out_cols + ff_cols :])
    mask_rows = learned_gate_scores.shape[0]
    logits_sum = columns(small_full[:, :, :mask_rows]).astype(f32) + columns(
        small_full[:, :, mask_rows : 2 * mask_rows]
    ).astype(f32)
    natural_log_gate = jax.nn.log_sigmoid(logits_sum / relaxation_heat[0])
    vectors_full = (
        small_full[:, 0, 2 * mask_rows : 2 * mask_rows + 8, :shard_rows]
        .transpose(1, 0, 2)
        .reshape(8, D)
        .astype(f32)
    )
    gains_full = vectors_full[:2]
    shifts_full = vectors_full[2:]
    bias_up = small_full[0, :, 2 * mask_rows + 8 :].reshape(1, -1).astype(f32)

    flat_in = layer_activations.reshape(row_count, D)
    qkv_bias = jnp.concatenate([shifts_full[0], jnp.zeros((D,), f32), shifts_full[1]])
    proj_low = (dot(flat_in, full_qkv) + qkv_bias).astype(bf16)
    head_shape = (seq_count, SEQ_LEN, HEADS, HEAD_DIM)
    queries = proj_low[:, :D].reshape(head_shape)
    keys_low = proj_low[:, D : 2 * D].reshape(head_shape)
    values_low = proj_low[:, 2 * D :].reshape(head_shape)
    live = lax.broadcasted_iota(jnp.int32, (seq_count, SEQ_LEN), 1) < token_counts_each[:, None]
    attended = [
        attend(queries[s], keys_low[s], values_low[s], natural_log_gate, live[s])
        for s in range(seq_count)
    ]
    context_low = jnp.concatenate(
        [item[0].reshape(SEQ_LEN, D).astype(bf16) for item in attended], axis=0
    )
    first_sum = flat_in.astype(f32) + dot(context_low, full_out) + shifts_full[2]
    hidden, normed_one, inv_one = layer_norm(first_sum, gains_full[0], shifts_full[4])
    hidden_low = hidden.astype(bf16)
    pre_act = dot(hidden_low, full_up) + bias_up
    act_low = jax.nn.gelu(pre_act, approximate=False).astype(bf16)
    second_sum = hidden + dot_last(act_low, full_down_t) + shifts_full[3]
    result, normed_two, inv_two = layer_norm(second_sum, gains_full[1], shifts_full[5])
    cot_flat = loss_grad_result.reshape(row_count, D).astype(f32)
    grad_second, grad_gain_two, grad_shift_two = norm_back(
        cot_flat, normed_two, inv_two, gains_full[1]
    )
    grad_second_low = grad_second.astype(bf16)
    grad_w_down_t = dot_first(grad_second_low, act_low)
    grad_act = dot(grad_second_low, full_down_t)
    grad_pre = (grad_act * gelu_slope(pre_act)).astype(bf16)
    grad_bias_up = jnp.sum(grad_pre, axis=0, dtype=f32)
    grad_w_up = dot_first(hidden_low, grad_pre)
    grad_hidden = grad_second + dot_last(grad_pre, full_up)
    grad_first, grad_gain_one, grad_shift_one = norm_back(
        grad_hidden, normed_one, inv_one, gains_full[0]
    )
    grad_first_low = grad_first.astype(bf16)
    grad_w_out = dot_first(context_low, grad_first_low)
    grad_context = dot_last(grad_first_low, full_out).astype(bf16).reshape(head_shape)
    back = [
        attend_back(
            queries[s],
            keys_low[s],
            values_low[s],
            natural_log_gate,
            live[s],
            attended[s][1],
            grad_context[s],
        )
        for s in range(seq_count)
    ]
    grad_mask = sum(item[3] for item in back)
    grad_projected = jnp.concatenate(
        [
            jnp.concatenate(
                [item[part].reshape(SEQ_LEN, D).astype(bf16) for item in back], axis=0
            )
            for part in range(3)
        ],
        axis=1,
    )
    grad_w_qkv = dot_first(flat_in, grad_projected)
    grad_inputs = grad_first + dot_last(grad_projected, full_qkv)
    grad_vectors = jnp.stack(
        [
            grad_gain_one,
            grad_gain_two,
            jnp.sum(grad_projected[:, :D], axis=0, dtype=f32),
            jnp.sum(grad_projected[:, 2 * D :], axis=0, dtype=f32),
            jnp.sum(grad_first, axis=0),
            jnp.sum(grad_second, axis=0),
            grad_shift_one,
            grad_shift_two,
        ]
    )
    big = jnp.concatenate(
        [
            blocks_of(item, rows_dp, cols_ffn)
            for item in (grad_w_qkv, grad_w_out, grad_w_up, grad_w_down_t)
        ],
        axis=-1,
    ).reshape(rows_dp * cols_ffn, shard_rows, -1)
    vector_blocks = jnp.broadcast_to(
        grad_vectors.reshape(8, rows_dp, 1, shard_rows).transpose(1, 2, 0, 3),
        (rows_dp, cols_ffn, 8, shard_rows),
    )
    bias_blocks = jnp.broadcast_to(
        grad_bias_up.reshape(1, cols_ffn, -1, mask_cols),
        (rows_dp, cols_ffn, ff_cols // mask_cols, mask_cols),
    )
    little = jnp.concatenate(
        [
            blocks_of(grad_mask, rows_dp, cols_ffn),
            jnp.pad(vector_blocks, ((0, 0), (0, 0), (0, 0), (0, mask_cols - shard_rows))),
            bias_blocks,
        ],
        axis=2,
    ).reshape(rows_dp * cols_ffn, -1, mask_cols)
    big = lax.psum_scatter(big, AXES, scatter_dimension=0, tiled=True)[0]
    little = lax.psum_scatter(little, AXES, scatter_dimension=0, tiled=True)[0]

    own_mixed = (
        learned_gate_scores.astype(f32) + fixed_jitter_matrix.astype(f32)
    ) / relaxation_heat[0]
    grad_logits = little[:mask_rows] * (jax.nn.sigmoid(-own_mixed) / relaxation_heat[0])
    return (
        result.astype(bf16).reshape(layer_activations.shape),
        grad_inputs.reshape(layer_activations.shape),
        big[:, :qkv_cols],
        big[:, qkv_cols : qkv_cols + out_cols],
        big[:, qkv_cols + out_cols : qkv_cols + out_cols + ff_cols],
        little[mask_rows + 8 :].reshape(-1),
        big[:, qkv_cols + out_cols + ff_cols :].T,
        little[mask_rows : mask_rows + 2, :shard_rows],
        little[mask_rows + 2 : mask_rows + 8, :shard_rows],
        grad_logits,
    )


def solution(mesh):
    in_specs = (
        P(AXES, None, None),
        P(AXES),
        P("dp", "ffn"),
        P("dp", "ffn"),
        P("dp", "ffn"),
        P("ffn"),
        P("ffn", "dp"),
        P(None, "dp"),
        P(None, "dp"),
        P("dp", "ffn"),
        P("dp", "ffn"),
        P(),
        P(AXES, None, None),
    )
    out_specs = (
        P(AXES, None, None),
        P(AXES, None, None),
        P("dp", "ffn"),
        P("dp", "ffn"),
        P("dp", "ffn"),
        P("ffn"),
        P("ffn", "dp"),
        P(None, "dp"),
        P(None, "dp"),
        P("dp", "ffn"),
    )
    return jax.shard_map(
        on_device, mesh=mesh, in_specs=in_specs, out_specs=out_specs, check_vma=False
    )
```

time: 1710 us -> 872 us (0.51)
  waiting for transfers between devices: 976 us -> 404 us
  blocking collectives: 313 us -> 0 us
  local copies, waits for them, and re-layouts: 92 us -> 195 us
  other arithmetic: 78.4 us -> 43.5 us
  starting transfers between devices: 25.4 us -> 0.16 us
    reduce_scatter x7 -> x2, waiting for transfers between devices: 702 us -> 255 us  [the longest x1 255 us: on_device(): big = lax.psum_scatter(big, AXES, scatter_dimension=0, tiled=True)[0]]
    all_gather x4 -> x0, blocking collectives: 273 us -> none  [the longest x1 70.6 us: fetch_weights(): lax.all_gather(learned_gate_scores[None], ('dp', 'ffn'), axis=0, tiled=True)]
    all_gather x8 -> x2, waiting for transfers between devices: 228 us -> 150 us  [the longest x1 95 us: gather_weights(): full = lax.all_gather(pack[None], AXES, axis=0, tiled=True)]
    concatenate x0 -> x4, local copies, waits for them, and re-layouts: none -> 73.7 us  [the longest x2 70.6 us: on_device(): jnp.concatenate([blocks_of(item, rows_dp, cols_ffn) for item in (grad_w_q...]
    all_to_all x6 -> x0, waiting for transfers between devices: 43.4 us -> none  [summed_on_arrival(): lax.all_to_all(parts, axis, split_axis=0, concat_axis=0, tiled=True)]
    unnamed x1 -> x0, blocking collectives: 39.7 us -> none
    reshape x7, local copies, waits for them, and re-layouts: 17.4 us -> 50.8 us  [the longest x4 40.9 us: blocks_of(): full.reshape(rows_dp, rows // rows_dp, cols_ffn, cols // cols_ffn)]
    all_to_all x6 -> x0, starting transfers between devices: 24.3 us -> none  [summed_on_arrival(): lax.all_to_all(parts, axis, split_axis=0, concat_axis=0, tiled=True)]
  transfers between devices with their start and end apart: 22 -> 4, of which waited for: 16 -> 3; matrix products, arithmetic and copies ran while one was open for 15% -> 19% of each run, Pallas kernels for 0% -> 0%
where the time goes in v1:
time: 872 us; the launch traced here: 861 us
  waiting for transfers between devices  404 us (46%)
  matrix products  203 us (23%)
  local copies, waits for them, and re-layouts  195 us (22%)
  other arithmetic  43.5 us (5%)
  between operations  15.8 us (2%)
    reduce_scatter x1, waiting for transfers between devices, on_device(): big = lax.psum_scatter(big, AXES, scatter_dimension=0, tiled=True)[0]  255 us
    all_gather x1, waiting for transfers between devices, gather_weights(): full = lax.all_gather(pack[None], AXES, axis=0, tiled=True)  95 us
    concatenate x2, local copies, waits for them, and re-layouts, on_device(): jnp.concatenate([blocks_of(item, rows_dp, cols_ffn) for item in (grad_w_q...  70.6 us
    dot_general x4, matrix products, dot(): return jnp.dot(left, right, preferred_element_type=f32)  59.7 us
    all_gather x1, waiting for transfers between devices, gather_weights(): small_full = lax.all_gather(small[None], AXES, axis=0, tiled=True)  54.8 us
    dot_general x4, matrix products, dot_first(): lax.dot_general(left, right, (((0,), (0,)), ((), ())), preferred_element_...  53.4 us
    dot_general x4, matrix products, dot_last(): lax.dot_general(left, right, (((1,), (1,)), ((), ())), preferred_element_...  43.2 us
    reshape x4, local copies, waits for them, and re-layouts, blocks_of(): full.reshape(rows_dp, rows // rows_dp, cols_ffn, cols // cols_ffn)  40.9 us
  transfers between devices with their start and end apart: 4, of which 3 were waited for; matrix products, arithmetic and copies ran while one was open for 19% of the time, Pallas kernels for 0%

profile of v1, /device:TPU:0, one launch (start us, length us, event | category | flops | bytes accessed | tf_op | source)
XLA Modules:
  0.0 861.3 jit_solution(12025389899913185391)
XLA Ops:
  7.9 1.4 maximum_bitcast_fusion
  9.4 1.9 concatenate.34
  13.4 54.8 %all-gather.8.cloned.1.call-done = bf16[32,142,128]{2,1,0:T(8,128)(2,1)} async-done(((bf16[1,142,128]{2,1,0:T(8,128)(2,1)}), bf16[32,142,128]{2,1,0:T(8,128)(2,1)}) %all-gather.8.cloned.1.call-update) | async-done | bytes 1163280 | tf_op jit(solution)/shard_map/all_gather | solution.py:96
  71.2 1.4 negate_bitcast_fusion
  73.9 1.3 copy.71
  78.7 95.0 %all-gather.6.cloned.1.call-done = bf16[3072,2304]{1,0:T(8,128)(2,1)} async-done(((bf16[96,2304]{1,0:T(8,128)(2,1)}), bf16[3072,2304]{1,0:T(8,128)(2,1)}) %all-gather.6.cloned.1.call-update) | async-done | bytes 14155792 | tf_op jit(solution)/shard_map/all_gather | solution.py:94
  173.8 6.8 fusion.75
  180.5 2.4 slice.200
  183.0 4.4 slice.186
  187.4 3.6 copy.98
  191.0 3.2 copy.101
  195.4 2.1 reshape.277
  197.6 6.0 copy.106
  203.6 6.5 reshape.274
  210.1 7.5 fusion.28
  217.7 1.5 fusion.76
  219.2 3.8 fusion.78
  223.0 1.9 fusion.17
  226.1 1.4 copy-done.1
  227.5 2.7 fusion.47
  230.2 3.8 fusion.79
  234.0 1.9 fusion.16
  237.1 1.4 copy-done
  238.6 2.9 fusion.48
  241.5 1.6 fusion.80
  244.1 3.6 copy.99
  249.9 35.1 %fusion.2 = (bf16[1024,3072]{1,0:T(8,128)(2,1)}, f32[1024,3072]{1,0:T(8,128)}) fusion(f32[3072]{0:T(1024)S(1)} %copy-done.48, bf16[768,3072]{1,0:T(8,128)(2,1)S(1)} %bitcast.199, f32[1024,768]{1,0:T(8,128)S(1)} %get-tuple-element.54, f32[768]{0:T(1024)S(1)} %add.180, f32[768]{0:T(1024)S(1)} %mul.179, f32[1024]{0:T(1024)S(1)} %add_rsqrt_fusion.1, ...), kind=kOutput, calls=%fused_computation.4 | convolution fusion | flops 5043388416 | bytes 26765312 | tf_op jit(solution)/shard_map/dot_general | solution.py:25
  285.1 7.8 fusion.81
  294.8 2.3 fusion.72
  297.1 15.4 %convert_reduce_fusion = (f32[3072]{0:T(1024)}, bf16[1024,3072]{1,0:T(8,128)(2,1)}) fusion(f32[1024,3072]{1,0:T(8,128)} %get-tuple-element.56, f32[3072]{0:T(1024)S(1)} %copy-done.48, bf16[768,3072]{1,0:T(8,128)(2,1)S(1)} %bitcast.204, f32[1024,768]{1,0:T(8,128)S(1)} %get-tuple-element.29), kind=kOutput, calls=%fused_computation.11 | convolution fusion | flops 4873516032 | bytes 26763264 | tf_op jit(solution)/shard_map/dot_general | solution.py:25
  312.5 9.9 %multiply_reduce_fusion.2 = (f32[768]{0:T(1024)S(1)}, f32[1024]{0:T(1024)S(1)}, f32[1024]{0:T(1024)S(1)}, f32[768]{0:T(1024)S(1)}, f32[1024,768]{1,0:T(8,128)}) fusion(f32[1024,768]{1,0:T(8,128)S(1)} %get-tuple-element.54, f32[1024]{0:T(1024)S(1)} %add_rsqrt_fusion.1, f32[1024]{0:T(1024)S(1)} %broadcast_multiply_fusion.4, f32[768]{0:T(1024)S(1)} %mul.179, ...), kind=kOutput, calls=%fused_computation.71 | convolution fusion | flops 4839698432 | bytes 20472832 | tf_op jit(solution)/shard_map/dot_general | solution.py:21
  322.4 2.8 fusion.74
  325.3 1.5 convolution_convert_fusion
  328.7 3.0 fusion.44
  331.7 8.5 multiply_reduce_fusion
  340.2 4.1 fusion.41
  344.3 8.4 multiply_reduce_fusion.1
  352.7 11.2 %fusion.31 = (f32[512,512]{0,1:T(8,128)}, bf16[12,512,512]{1,2,0:T(8,128)(2,1)}) fusion(f32[12,512,512]{1,2,0:T(8,128)} %get-tuple-element.61, f32[12,512]{1,0:T(8,128)S(1)} %get-tuple-element.60, f32[12,512,512]{1,2,0:T(8,128)S(1)} %bitcast.167, f32[12,512]{1,0:T(8,128)S(1)} %copy-done.40), kind=kLoop, calls=%fused_computation.56 | loop fusion | flops 15466496 | bytes 32555008 | tf_op jit(solution)/shard_map/reduce_sum | solution.py:80
  364.0 4.9 multiply_convert_fusion
  370.1 7.4 fusion.29
  377.5 2.0 multiply_convert_fusion.1
  382.2 2.8 fusion.56
  385.7 29.6 %convolution_bitcast_fusion = f32[768,2304]{0,1:T(8,128)} fusion(bf16[1024,768]{1,0:T(8,128)(2,1)S(1)} %bitcast.240, bf16[512,768]{0,1:T(8,128)(2,1)S(1)} %bitcast.212, bf16[512,768]{0,1:T(8,128)(2,1)S(1)} %bitcast.215, bf16[512,768]{0,1:T(8,128)(2,1)S(1)} %bitcast.228, bf16[512,768]{0,1:T(8,128)(2,1)S(1)} %bitcast.230, bf16[512,768]{0,1:T(8,128)(2,1)S(1)} %bitcast.190, ...), kind=kOutput, calls=%fused_computation.50 | convolution fusion | flops 3652190208 | bytes 13369344 | tf_op jit(solution)/shard_map/dot_general | solution.py:17
  415.2 8.0 copy.83
  423.3 10.4 %reshape.282 = f32[8,96,4,576]{3,2,1,0:T(4,128)} reshape(f32[768,2304]{1,0:T(8,128)} %copy.83) | data formatting | bytes 14155776 | tf_op jit(solution)/shard_map/reshape | solution.py:107
  433.7 5.2 reshape.283
  439.7 1.3 copy.85
  441.0 2.7 add.200
  443.9 1.5 fusion.49
  446.7 10.6 %fusion.68 = f32[768,3072]{1,0:T(8,128)} fusion(bf16[1024,3072]{1,0:T(8,128)(2,1)} %get-tuple-element.65, f32[1024,768]{1,0:T(8,128)S(1)} %copy-done.4, f32[768]{0:T(1024)S(1)} %add.180, f32[768]{0:T(1024)S(1)} %mul.179, f32[1024]{0:T(1024)S(1)} %add_rsqrt_fusion.1, f32[1024]{0:T(1024)S(1)} %broadcast_multiply_fusion.4), kind=kOutput, calls=%fused_computation.152 | convolution fusion | flops 4835770368 | bytes 18888704 | tf_op jit(solution)/shard_map/dot_general | solution.py:17
  457.3 12.7 %reshape.284 = f32[8,96,4,768]{3,2,1,0:T(4,128)} reshape(f32[768,3072]{1,0:T(8,128)} %fusion.68) | data formatting | bytes 18874368 | tf_op jit(solution)/shard_map/reshape | solution.py:107
  470.0 10.4 %fusion.59 = f32[768,3072]{1,0:T(8,128)} fusion(bf16[1024,3072]{1,0:T(8,128)(2,1)} %get-tuple-element.55, f32[1024,768]{1,0:T(8,128)S(1)} %copy-done.22), kind=kOutput, calls=%fused_computation.113 | convolution fusion | flops 4832624640 | bytes 18874368 | tf_op jit(solution)/shard_map/dot_general | solution.py:17
  480.4 12.6 %reshape.285 = f32[8,96,4,768]{3,2,1,0:T(4,128)} reshape(f32[768,3072]{1,0:T(8,128)} %fusion.59) | data formatting | bytes 18874368 | tf_op jit(solution)/shard_map/reshape | solution.py:107
  493.0 46.2 %concatenate.43 = f32[8,4,96,2304]{3,1,2,0:T(4,128)} concatenate(f32[8,4,96,576]{3,1,2,0:T(4,128)} %bitcast.171, f32[8,4,96,192]{3,1,2,0:T(4,128)S(1)} %bitcast.180, f32[8,4,96,768]{3,1,2,0:T(4,128)} %bitcast.169, f32[8,4,96,768]{3,1,2,0:T(4,128)} %bitcast.170), dimensions={3} | concatenate | bytes 56623104 | tf_op jit(solution)/shard_map/concatenate | solution.py:249
  539.2 24.4 %copy.84 = f32[8,4,96,2304]{3,2,1,0:T(8,128)} copy(f32[8,4,96,2304]{3,1,2,0:T(4,128)} %concatenate.43) | data formatting | bytes 56623104 | tf_op jit(solution)/shard_map/concatenate | solution.py:249
  565.5 24.0 %convolution_add_fusion.1 = f32[1024,768]{1,0:T(8,128)} fusion(f32[1024,768]{1,0:T(8,128)} %copy-done.27, bf16[768,2304]{1,0:T(8,128)(2,1)} %copy-done.18, bf16[512,768]{0,1:T(8,128)(2,1)S(1)} %bitcast.213, bf16[512,768]{0,1:T(8,128)(2,1)S(1)} %bitcast.216, bf16[512,768]{0,1:T(8,128)(2,1)} %bitcast.229, bf16[512,768]{0,1:T(8,128)(2,1)} %bitcast.231, ...), kind=kOutput, calls=%fused_computation.88 | convolution fusion | flops 3652976640 | bytes 14548992 | tf_op jit(solution)/shard_map/dot_general | solution.py:21
  589.4 1.2 slice.217
  590.7 1.3 slice.218
  591.9 1.3 slice_bitcast_fusion.3
  593.2 1.4 fusion.62
  594.6 254.5 %reduce-scatter.3.cloned.1.call-done = f32[1,96,2304]{2,1,0:T(8,128)} async-done(((f32[32,96,2304]{2,1,0:T(8,128)}), f32[1,96,2304]{2,1,0:T(8,128)}) %reduce-scatter.3.cloned.1.call-update) | async-done | bytes 884752 | tf_op jit(solution)/shard_map/reduce_scatter | solution.py:272
  849.1 1.7 slice.212
  850.8 1.6 slice.213
  852.4 1.9 slice_bitcast_fusion
  (207 shorter events, 28.7 us)
Async XLA Ops:
  7.2 61.0 %all-gather.8.cloned.1.call-start = ((), (), s32[]{:S(2)}) async-start(), calls=%async_computation.5 | async-start | bytes 1216512 | tf_op jit(solution)/shard_map/all_gather | solution.py:96
  9.3 164.4 %all-gather.6.cloned.1.call-start = ((), (), s32[]{:S(2)}) async-start(), calls=%async_computation.4 | async-start | bytes 14598144 | tf_op jit(solution)/shard_map/all_gather | solution.py:94
  11.3 64.1 %copy-start.5 = (bf16[2,512,768]{2,1,0:T(8,128)(2,1)S(1)}, bf16[2,512,768]{2,1,0:T(8,128)(2,1)}, u32[]{:S(2)}) copy-start(bf16[2,512,768]{2,1,0:T(8,128)(2,1)} %param.25) | copy-start | bytes 4718596
  11.3 578.1 %reduce-scatter.5.cloned.1.call-start = ((), (), s32[]{:S(2)}) async-start(), calls=%async_computation.3 | async-start | bytes 1351680 | tf_op jit(solution)/shard_map/reduce_scatter | solution.py:273
  75.4 105.1 %copy-start.41 = (f32[768]{0:T(1024)}, f32[768]{0:T(1024)S(1)}, u32[]{:S(2)}) copy-start(f32[768]{0:T(1024)S(1)} %mul.188) | copy-start | bytes 9220
  210.1 7.6 copy-start.18
  219.1 3.9 copy-start.11
  219.1 3.9 copy-start.31
  219.1 11.1 %copy-start.9 = (bf16[512,768]{0,1:T(8,128)(2,1)}, bf16[512,768]{0,1:T(8,128)(2,1)S(1)}, u32[]{:S(2)}) copy-start(bf16[512,768]{0,1:T(8,128)(2,1)S(1)} %get-tuple-element.38) | copy-start | bytes 2359300
  219.1 18.0 %copy-start.19 = (bf16[512,768]{0,1:T(8,128)(2,1)}, bf16[512,768]{0,1:T(8,128)(2,1)S(1)}, u32[]{:S(2)}) copy-start(bf16[512,768]{0,1:T(8,128)(2,1)S(1)} %get-tuple-element.43) | copy-start | bytes 2359300
  223.0 4.5 copy-start.1
  223.0 4.5 copy-start.20
  227.5 2.7 copy-start.29
  227.5 2.7 copy-start.36
  230.2 11.3 %copy-start.54 = (bf16[12,64,512]{2,1,0:T(8,128)(2,1)}, bf16[12,64,512]{2,1,0:T(8,128)(2,1)S(1)}, u32[]{:S(2)}) copy-start(bf16[12,64,512]{2,1,0:T(8,128)(2,1)S(1)} %fusion.47) | copy-start | bytes 2359300
  234.0 4.5 copy-start
  238.6 2.9 copy-start.33
  238.6 2.9 copy-start.52
  241.5 2.5 slice-start.6
  241.5 2.6 slice-start.7
  243.1 79.3 %copy-start.3 = (f32[1024,768]{1,0:T(8,128)}, f32[1024,768]{1,0:T(8,128)S(1)}, u32[]{:S(2)}) copy-start(f32[1024,768]{1,0:T(8,128)S(1)} %get-tuple-element.54) | copy-start | bytes 9437188
  244.1 4.7 slice-start.8
  247.7 2.2 slice-start.9
  247.7 2.2 copy-start.48
  249.9 35.1 %copy-start.50 = (f32[768]{0:T(1024)S(1)}, f32[768]{0:T(1024)}, u32[]{:S(2)}) copy-start(f32[768]{0:T(1024)} %add.186) | copy-start | bytes 9220
  285.0 8.4 copy-start.6
  285.0 8.4 copy-start.42
  294.8 17.7 %slice-start.10 = ((s8[4718592]{0:T(1024)(128)(4,1)}), s8[4194304]{0:T(1024)(128)(4,1)S(1)}, s32[]{:S(2)}) async-start(s8[4718592]{0:T(1024)(128)(4,1)} %bitcast.200), calls=%async_computation.16 | async-start | bytes 8388608
  297.1 15.4 %copy-start.21 = (f32[1024,768]{1,0:T(8,128)}, f32[1024,768]{1,0:T(8,128)S(1)}, u32[]{:S(2)}) copy-start(f32[1024,768]{1,0:T(8,128)S(1)} %get-tuple-element.29) | copy-start | bytes 9437188
  297.1 15.4 %slice-start.11 = ((s8[4718592]{0:T(1024)(128)(4,1)}), s8[524288]{0:T(1024)(128)(4,1)S(1)}, s32[]{:S(2)}) async-start(s8[4718592]{0:T(1024)(128)(4,1)} %bitcast.200), calls=%async_computation.17 | async-start | bytes 1048576
  297.1 31.6 %slice-start.3 = ((s8[12582912]{0:T(1024)(128)(4,1)}), s8[4194304]{0:T(1024)(128)(4,1)S(1)}, s32[]{:S(2)}) async-start(s8[12582912]{0:T(1024)(128)(4,1)} %bitcast.166), calls=%async_computation.9 | async-start | bytes 8388608
  297.1 31.6 %slice-start.4 = ((s8[12582912]{0:T(1024)(128)(4,1)}), s8[4194304]{0:T(1024)(128)(4,1)S(1)}, s32[]{:S(2)}) async-start(s8[12582912]{0:T(1024)(128)(4,1)} %bitcast.166), calls=%async_computation.10 | async-start | bytes 8388608
  312.5 16.2 %slice-start.5 = ((s8[12582912]{0:T(1024)(128)(4,1)}), s8[4194304]{0:T(1024)(128)(4,1)S(1)}, s32[]{:S(2)}) async-start(s8[12582912]{0:T(1024)(128)(4,1)} %bitcast.166), calls=%async_computation.11 | async-start | bytes 8388608
  322.4 2.9 copy-start.34
  325.3 2.5 copy-start.27
  325.3 3.4 copy-start.40
  328.7 11.5 %slice-start = ((s8[12582912]{0:T(1024)(128)(4,1)}), s8[4194304]{0:T(1024)(128)(4,1)S(1)}, s32[]{:S(2)}) async-start(s8[12582912]{0:T(1024)(128)(4,1)} %bitcast.164), calls=%async_computation.6 | async-start | bytes 8388608
  328.7 11.5 %slice-start.1 = ((s8[12582912]{0:T(1024)(128)(4,1)}), s8[4194304]{0:T(1024)(128)(4,1)S(1)}, s32[]{:S(2)}) async-start(s8[12582912]{0:T(1024)(128)(4,1)} %bitcast.164), calls=%async_computation.7 | async-start | bytes 8388608
  331.7 8.5 slice-start.2
  331.7 8.5 copy-start.39
  352.7 11.3 %copy-start.32 = (bf16[512,768]{0,1:T(8,128)(2,1)S(1)}, bf16[512,768]{0,1:T(8,128)(2,1)}, u32[]{:S(2)}) copy-start(bf16[512,768]{0,1:T(8,128)(2,1)} %copy-done.31) | copy-start | bytes 2359300
  363.9 4.9 copy-start.2
  363.9 5.0 copy-start.12
  368.9 16.7 %copy-start.37 = (bf16[12,64,512]{2,1,0:T(8,128)(2,1)}, bf16[12,64,512]{2,1,0:T(8,128)(2,1)S(1)}, u32[]{:S(2)}) copy-start(bf16[12,64,512]{2,1,0:T(8,128)(2,1)S(1)} %multiply_convert_fusion) | copy-start | bytes 2359300
  370.1 15.6 %copy-start.13 = (bf16[12,64,512]{2,1,0:T(8,128)(2,1)}, bf16[12,64,512]{2,1,0:T(8,128)(2,1)S(1)}, u32[]{:S(2)}) copy-start(bf16[12,64,512]{2,1,0:T(8,128)(2,1)S(1)} %multiply_convert_fusion.2) | copy-start | bytes 2359300
  370.1 7.5 copy-start.30
  377.5 2.0 copy-start.10
  379.6 6.1 copy-start.38
  379.6 2.2 copy-start.28
  379.6 2.4 copy-start.55
  379.6 2.6 copy-start.57
  382.2 3.5 copy-start.15
  382.2 3.1 copy-start.23
  382.2 3.1 copy-start.25
  382.2 3.5 copy-start.53
  433.7 5.8 copy-start.49
  433.7 5.8 copy-start.17
  438.9 4.9 copy-start.47
  441.0 5.7 copy-start.4
  446.6 402.5 %reduce-scatter.3.cloned.1.call-start = ((), (), s32[]{:S(2)}) async-start(), calls=%async_computation.2 | async-start | bytes 29196288 | tf_op jit(solution)/shard_map/reduce_scatter | solution.py:272
  457.3 12.7 %copy-start.22 = (f32[1024,768]{1,0:T(8,128)S(1)}, f32[1024,768]{1,0:T(8,128)}, u32[]{:S(2)}) copy-start(f32[1024,768]{1,0:T(8,128)} %copy-done.21) | copy-start | bytes 9437188
  480.4 12.6 %copy-start.7 = (f32[8,96,4,192]{3,2,1,0:T(4,128)S(1)}, f32[8,96,4,192]{3,2,1,0:T(4,128)}, u32[]{:S(2)}) copy-start(f32[8,96,4,192]{3,2,1,0:T(4,128)} %reshape.283) | copy-start | bytes 7077892
  565.5 27.8 %copy-start.43 = (bf16[64,128]{1,0:T(8,128)(2,1)S(1)}, bf16[64,128]{1,0:T(8,128)(2,1)}, u32[]{:S(2)}) copy-start(bf16[64,128]{1,0:T(8,128)(2,1)} %param.23) | copy-start | bytes 49156
  565.5 27.8 %copy-start.44 = (bf16[64,128]{1,0:T(8,128)(2,1)S(1)}, bf16[64,128]{1,0:T(8,128)(2,1)}, u32[]{:S(2)}) copy-start(bf16[64,128]{1,0:T(8,128)(2,1)} %param.22) | copy-start | bytes 49156
  (10 other events, 15.2 us)
Sparse Core Ops, SparseCore 0:
  11.4 56.7 all-gather.7
  71.6 102.1 all-gather.5
  446.7 134.5 reduce-scatter.4
  588.8 260.3 reduce-scatter.2

commit v2 on v1

--- a/solution.py
+++ b/solution.py
@@ -1,6 +1,8 @@
 import jax
 import jax.numpy as jnp
 from jax import lax
+from jax.experimental import pallas as pl
+from jax.experimental.pallas import tpu as pltpu
 from jax.sharding import PartitionSpec as P
 
 D = 768
@@ -11,6 +13,7 @@
 norm_eps = 1e-06
 f32 = jnp.float32
 bf16 = jnp.bfloat16
+MESH = pl.DeviceIdType.MESH
 
 
 def dot_first(left, right):
@@ -88,9 +91,242 @@
     return (grad_queries, grad_keys, grad_values, grad_mask)
 
 
+def partners():
+    i = lax.axis_index("dp"); f = lax.axis_index("ffn")
+    c = i % 2
+    x = (i // 2) % 2
+    core = i + 1 - 2 * c
+    ix = i + 2 - 4 * x
+    iy = (i + 4) % 8
+    idg = (ix + 4) % 8
+    return i, f, core, ix, iy, idg
+
+class Gather:
+    NS = 19
+    def __init__(self, src, dst, ssem, rsem, lsem):
+        self.src, self.dst, self.ssem, self.rsem, self.lsem = src, dst, ssem, rsem, lsem
+        self.rows = src.shape[0]
+        self.me = partners()
+        self.pending = []
+    def piece(self, i, p):
+        return self.dst.at[p, pl.ds(i * self.rows, self.rows)]
+    def block(self, i):
+        return self.dst.at[:, pl.ds(i * self.rows, self.rows)]
+    def remote(self, src, dst, n, to):
+        return pltpu.make_async_remote_copy(src_ref=src, dst_ref=dst, send_sem=self.ssem.at[n], recv_sem=self.rsem.at[n], device_id=to, device_id_type=MESH)
+    def send(self, src, dst, n, to):
+        cp = self.remote(src, dst, n, to)
+        cp.start()
+        self.pending.append(cp)
+    def recv(self, ref, n):
+        i, f, *_ = self.me
+        self.remote(ref, ref, n, (i, f)).wait_recv()
+    def s0(self):
+        i, f, core, ix, iy, idg = self.me
+        own = self.piece(i, f)
+        cp = pltpu.make_async_copy(self.src, own, self.lsem)
+        cp.start()
+        self.local = cp
+        for k in (1, 2, 3):
+            self.send(self.src, own, 3 - k, (i, (f + k) % 4))
+        self.send(self.src, own, 3, (ix, f))
+        self.send(self.src, own, 7, (iy, f))
+    def s1(self):
+        i, f, core, ix, iy, idg = self.me
+        for k in (1, 2, 3):
+            p = (f + k) % 4
+            ref = self.piece(i, p)
+            self.recv(ref, k - 1)
+            self.send(ref, ref, 3 + k, (ix, f))
+            self.send(ref, ref, 7 + k, (iy, f))
+        self.local.wait()
+        blk = self.block(i)
+        self.send(blk, blk, 15, (core, f))
+    def s2(self):
+        i, f, core, ix, iy, idg = self.me
+        for k in range(4):
+            p = (f + k) % 4
+            rx = self.piece(ix, p); ry = self.piece(iy, p)
+            self.recv(rx, 3 + k)
+            if k % 2: self.send(rx, rx, 11 + k, (iy, f))
+            self.recv(ry, 7 + k)
+            if k % 2 == 0: self.send(ry, ry, 11 + k, (ix, f))
+        bx = self.block(ix); by = self.block(iy)
+        self.send(bx, bx, 16, (core, f))
+        self.send(by, by, 17, (core, f))
+    def s3(self):
+        i, f, core, ix, iy, idg = self.me
+        for k in range(4):
+            self.recv(self.piece(idg, (f + k) % 4), 11 + k)
+        b = self.block(idg)
+        self.send(b, b, 18, (core, f))
+    def s4(self):
+        i, f, core, ix, iy, idg = self.me
+        co = lambda v: v + 1 - 2 * (i % 2)
+        for n, b in ((15, i), (16, ix), (17, iy), (18, idg)):
+            self.recv(self.block(co(b)), n)
+    def finish(self):
+        for cp in self.pending:
+            cp.wait_send()
+
+def barrier():
+    i, f, core, ix, iy, idg = partners()
+    b = pltpu.get_barrier_semaphore()
+    for to in ((i, (f + 1) % 4), (i, (f + 2) % 4), (i, (f + 3) % 4), (core, f), (ix, f), (iy, f)):
+        pl.semaphore_signal(b, inc=1, device_id=to, device_id_type=MESH)
+    pl.semaphore_wait(b, 6)
+
+def ag_kernel(pack, small, wfull, sfull, ssem, rsem, lsem):
+    barrier()
+    gs = [Gather(small, sfull, ssem.at[0], rsem.at[0], lsem.at[0])]
+    for g in range(3):
+        gs.append(Gather(pack.at[g], wfull.at[g], ssem.at[1 + g], rsem.at[1 + g], lsem.at[1 + g]))
+    S, A, U, Dn = gs
+    S.s0(); A.s0()
+    S.s1(); A.s1(); U.s0()
+    S.s2(); A.s2(); U.s1(); Dn.s0()
+    S.s3(); A.s3(); U.s2(); Dn.s1()
+    S.s4(); A.s4()
+    U.s3(); Dn.s2(); U.s4(); Dn.s3(); Dn.s4()
+    for g in gs: g.finish()
+
+def ag_call(pack, small):
+    _, rows, cols = pack.shape
+    srows, scols = small.shape
+    any_ = pl.BlockSpec(memory_space=pl.ANY)
+    return pl.pallas_call(
+        ag_kernel,
+        out_shape=(jax.ShapeDtypeStruct((3, 4, rows * 8, cols), bf16), jax.ShapeDtypeStruct((4, 8 * srows, scols), bf16)),
+        in_specs=[any_] * 2, out_specs=(any_, any_),
+        scratch_shapes=[pltpu.SemaphoreType.DMA((4, 19)), pltpu.SemaphoreType.DMA((4, 19)), pltpu.SemaphoreType.DMA((4,))],
+        compiler_params=pltpu.CompilerParams(collective_id=0, has_side_effects=True),
+        name="gather_weights",
+    )(pack, small)
+
+class Scatter:
+    NS = 19
+    def __init__(self, part, rc, rq, rx, ry, rz, out, ssem, rsem):
+        self.part, self.rc, self.rq, self.rx, self.ry, self.rz, self.out = part, rc, rq, rx, ry, rz, out
+        self.ssem, self.rsem = ssem, rsem
+        self.rows = part.shape[1] // 8
+        self.me = partners()
+        self.pending = []
+    def piece(self, i, p):
+        return self.part.at[p, pl.ds(pl.multiple_of(i * self.rows, self.rows), self.rows)]
+    def block(self, i):
+        return self.part.at[:, pl.ds(pl.multiple_of(i * self.rows, self.rows), self.rows)]
+    def send(self, src, dst, n, to):
+        cp = pltpu.make_async_remote_copy(src_ref=src, dst_ref=dst, send_sem=self.ssem.at[n], recv_sem=self.rsem.at[n], device_id=to, device_id_type=MESH)
+        cp.start()
+        self.pending.append(cp)
+    def recv(self, ref, n):
+        i, f, *_ = self.me
+        pltpu.make_async_remote_copy(src_ref=ref, dst_ref=ref, send_sem=self.ssem.at[n], recv_sem=self.rsem.at[n], device_id=(i, f), device_id_type=MESH).wait_recv()
+    def r0(self):
+        i, f, core, ix, iy, idg = self.me
+        d = core - i
+        for n, b in ((3, idg), (1, ix), (2, iy), (0, i)):
+            self.send(self.block(b + d), self.rc.at[n], n, (core, f))
+    def add_core(self, n, b, ks=(0, 1, 2, 3)):
+        f = self.me[1]
+        for k in ks:
+            p = (f + k) % 4
+            ref = self.piece(b, p)
+            ref[...] = (ref[...].astype(f32) + self.rc[n, p].astype(f32)).astype(ref.dtype)
+    def r1(self):
+        i, f, core, ix, iy, idg = self.me
+        self.recv(self.rc.at[3], 3)
+        self.add_core(3, idg)
+        for k in range(4):
+            self.send(self.piece(idg, (f + k) % 4), self.rq.at[k], 4 + k, (iy if k % 2 else ix, f))
+        self.recv(self.rc.at[1], 1)
+        self.add_core(1, ix)
+        for k in (0, 2):
+            self.send(self.piece(ix, (f + k) % 4), self.rx.at[k], 8 + k, (ix, f))
+        self.recv(self.rc.at[2], 2)
+        self.add_core(2, iy)
+        for k in (1, 3):
+            self.send(self.piece(iy, (f + k) % 4), self.ry.at[k], 12 + k, (iy, f))
+        self.recv(self.rc.at[0], 0)
+        self.add_core(0, i)
+    def r2(self):
+        i, f, core, ix, iy, idg = self.me
+        for k in range(4):
+            self.recv(self.rq.at[k], 4 + k)
+            b = ix if k % 2 else iy
+            ref = self.piece(b, (f + k) % 4)
+            ref[...] = (ref[...].astype(f32) + self.rq[k].astype(f32)).astype(ref.dtype)
+            if k % 2:
+                self.send(ref, self.rx.at[k], 8 + k, (ix, f))
+            else:
+                self.send(ref, self.ry.at[k], 12 + k, (iy, f))
+    def r3(self):
+        i, f, core, ix, iy, idg = self.me
+        for k in (1, 2, 3, 0):
+            self.recv(self.rx.at[k], 8 + k)
+            self.recv(self.ry.at[k], 12 + k)
+            ref = self.piece(i, (f + k) % 4)
+            total = ref[...].astype(f32) + self.rx[k].astype(f32) + self.ry[k].astype(f32)
+            if k:
+                ref[...] = total.astype(ref.dtype)
+                self.send(ref, self.rz.at[3 - k], 19 - k, (i, (f + k) % 4))
+            else:
+                self.out[...] = total
+    def r4(self):
+        for k in range(3):
+            self.recv(self.rz.at[k], 16 + k)
+        self.out[...] = self.out[...] + self.rz[0].astype(f32) + self.rz[1].astype(f32) + self.rz[2].astype(f32)
+    def finish(self):
+        for cp in self.pending:
+            cp.wait_send()
+
+def scatter_scratch(rows, cols, dt):
+    return [pltpu.VMEM((4, 4, rows, cols), dt), pltpu.VMEM((4, rows, cols), dt), pltpu.VMEM((4, rows, cols), dt), pltpu.VMEM((4, rows, cols), dt), pltpu.VMEM((3, rows, cols), dt)]
+
+def rs_kernel(big, little, obig, olit, part, lpart, rc, rq, rx, ry, rz, lrc, lrq, lrx, lry, lrz, ssem, rsem, lsem):
+    cps = []
+    for g, (s, d) in enumerate(((big.at[0], part.at[0]), (big.at[1], part.at[1]), (big.at[2], part.at[2]), (little, lpart))):
+        cp = pltpu.make_async_copy(s, d, lsem.at[g]); cp.start(); cps.append(cp)
+    barrier()
+    G = [Scatter(part.at[g], rc.at[g], rq.at[g], rx.at[g], ry.at[g], rz.at[g], obig.at[g], ssem.at[g], rsem.at[g]) for g in range(3)]
+    L = Scatter(lpart, lrc, lrq, lrx, lry, lrz, olit, ssem.at[3], rsem.at[3])
+    G.append(L)
+    for n in range(4 + 4):
+        for g in range(4):
+            st = n - g
+            if st == 0: cps[g].wait()
+            if 0 <= st <= 4: (G[g].r0, G[g].r1, G[g].r2, G[g].r3, G[g].r4)[st]()
+    for g in G: g.finish()
+
+def rs_call(big, little):
+    _, _, r8, cols = big.shape
+    rows = r8 // 8
+    lrows, lcols = little.shape[1] // 8, little.shape[2]
+    vm = pl.BlockSpec(memory_space=pltpu.VMEM)
+    any_ = pl.BlockSpec(memory_space=pl.ANY)
+    v3 = [pltpu.VMEM((3,) + s.shape, s.dtype) for s in [pltpu.VMEM((4, 4, rows, cols), bf16), pltpu.VMEM((4, rows, cols), bf16), pltpu.VMEM((4, rows, cols), bf16), pltpu.VMEM((4, rows, cols), bf16), pltpu.VMEM((3, rows, cols), bf16)]]
+    return pl.pallas_call(
+        rs_kernel,
+        out_shape=(jax.ShapeDtypeStruct((3, rows, cols), f32), jax.ShapeDtypeStruct((lrows, lcols), f32)),
+        in_specs=[any_, any_], out_specs=(vm, vm),
+        scratch_shapes=[pltpu.VMEM(big.shape, bf16), pltpu.VMEM(little.shape, f32)] + v3 + scatter_scratch(lrows, lcols, f32)
+            + [pltpu.SemaphoreType.DMA((4, 19)), pltpu.SemaphoreType.DMA((4, 19)), pltpu.SemaphoreType.DMA((4,))],
+        compiler_params=pltpu.CompilerParams(collective_id=1, has_side_effects=True, vmem_limit_bytes=60 << 20),
+        name="reduce_gradients",
+    )(big, little)
+
+
 def gather_weights(pack, small):
     rows_dp = lax.axis_size("dp")
     cols_ffn = lax.axis_size("ffn")
+    if (rows_dp, cols_ffn) == (8, 4):
+        rows, cols = pack.shape
+        packs = pack.reshape(rows, 3, cols // 3).transpose(1, 0, 2)
+        fill = -small.shape[0] % 16
+        full, small_full = ag_call(packs, jnp.pad(small, ((0, fill), (0, 0))))
+        full = full.reshape(3, 4, 8, rows, cols // 3).transpose(2, 1, 3, 0, 4)
+        small_full = small_full.reshape(4, 8, -1, small.shape[1]).transpose(1, 0, 2, 3)
+        return full.reshape(8, 4, rows, cols), small_full[:, :, : small.shape[0]]
     full = lax.all_gather(pack[None], AXES, axis=0, tiled=True)
     full = full.reshape(rows_dp, cols_ffn, *pack.shape)
     small_full = lax.all_gather(small[None], AXES, axis=0, tiled=True)
@@ -105,6 +341,24 @@
 def blocks_of(full, rows_dp, cols_ffn):
     rows, cols = full.shape
     return full.reshape(rows_dp, rows // rows_dp, cols_ffn, cols // cols_ffn).transpose(0, 2, 1, 3)
+
+
+def reduce_gradients(big, little, rows_dp, cols_ffn):
+    if (rows_dp, cols_ffn) == (8, 4):
+        rows, cols = big.shape[1:]
+        parts = big.astype(bf16).reshape(8, 4, rows, 3, cols // 3).transpose(3, 1, 0, 2, 4)
+        little_rows = little.shape[1]
+        little = jnp.pad(little, ((0, 0), (0, -little_rows % 8), (0, 0)))
+        little_parts = little.reshape(8, 4, *little.shape[1:]).transpose(1, 0, 2, 3)
+        big, little = rs_call(
+            parts.reshape(3, 4, 8 * rows, cols // 3),
+            little_parts.reshape(4, -1, little.shape[2]),
+        )
+        return big.transpose(1, 0, 2).reshape(rows, cols), little[:little_rows]
+    return (
+        lax.psum_scatter(big, AXES, scatter_dimension=0, tiled=True)[0],
+        lax.psum_scatter(little, AXES, scatter_dimension=0, tiled=True)[0],
+    )
 
 
 def on_device(
@@ -269,8 +523,7 @@
         ],
         axis=2,
     ).reshape(rows_dp * cols_ffn, -1, mask_cols)
-    big = lax.psum_scatter(big, AXES, scatter_dimension=0, tiled=True)[0]
-    little = lax.psum_scatter(little, AXES, scatter_dimension=0, tiled=True)[0]
+    big, little = reduce_gradients(big, little, rows_dp, cols_ffn)
 
     own_mixed = (
         learned_gate_scores.astype(f32) + fixed_jitter_matrix.astype(f32)

time: 872 us -> 640 us (0.73)
  waiting for transfers between devices: 404 us -> 0 us
  Pallas kernels: 0 us -> 165 us
  local copies, waits for them, and re-layouts: 195 us -> 254 us
  matrix products: 203 us -> 172 us
  between operations: 15.8 us -> 2.47 us
    reduce_scatter x2 -> x0, waiting for transfers between devices: 255 us -> none  [the longest x1 255 us: on_device(): big = lax.psum_scatter(big, AXES, scatter_dimension=0, tiled=True)[0]]
    pallas_call x0 -> x2, Pallas kernels: none -> 165 us  [the longest x1 87.5 us: rs_call(): pl.pallas_call(rs_kernel, out_shape=(jax.ShapeDtypeStruct((3, rows, cols)...]
    all_gather x2 -> x0, waiting for transfers between devices: 150 us -> none  [the longest x1 95 us: gather_weights(): full = lax.all_gather(pack[None], AXES, axis=0, tiled=True)]
    reshape x0 -> x5, local copies, waits for them, and re-layouts: none -> 60.2 us  [the longest x1 36.6 us: gather_weights(): return (full.reshape(8, 4, rows, cols), small_full[:, :, :small.shape[0]])]
    transpose x0 -> x11, local copies, waits for them, and re-layouts: none -> 55.3 us  [the longest x7 23.9 us: columns(): return blocks.transpose(0, 2, 1, 3).reshape(rows_dp * rows, cols_ffn * cols)]
    concatenate x2 -> x1, local copies, waits for them, and re-layouts: 70.6 us -> 21.6 us  [on_device(): jnp.concatenate([blocks_of(item, rows_dp, cols_ffn) for item in (grad_w_q...]
    convert_element_type x0 -> x1, local copies, waits for them, and re-layouts: none -> 31.2 us  [reduce_gradients(): big.astype(bf16).reshape(8, 4, rows, 3, cols // 3).transpose(3, 1, 0, 2, 4)]
    dot_general x4, matrix products: 43.2 us -> 22 us  [dot_last(): lax.dot_general(left, right, (((1,), (1,)), ((), ())), preferred_element_...]
  transfers between devices with their start and end apart: 4 -> 0, of which waited for: 3 -> 0; matrix products, arithmetic and copies ran while one was open for 19% -> 0% of each run, Pallas kernels for 0% -> 0%
where the time goes in v2:
time: 640 us; the launch traced here: 633 us
  local copies, waits for them, and re-layouts  254 us (40%)
  matrix products  172 us (27%)
  Pallas kernels  165 us (26%)
  other arithmetic  39.5 us (6%)
    pallas_call x1, Pallas kernels, rs_call(): pl.pallas_call(rs_kernel, out_shape=(jax.ShapeDtypeStruct((3, rows, cols)...  87.5 us
    pallas_call x1, Pallas kernels, ag_call(): pl.pallas_call(ag_kernel, out_shape=(jax.ShapeDtypeStruct((3, 4, rows * 8...  77.6 us
    dot_general x4, matrix products, dot(): return jnp.dot(left, right, preferred_element_type=f32)  55.1 us
    dot_general x4, matrix products, dot_first(): lax.dot_general(left, right, (((0,), (0,)), ((), ())), preferred_element_...  46.8 us
    reshape x1, local copies, waits for them, and re-layouts, gather_weights(): return (full.reshape(8, 4, rows, cols), small_full[:, :, :small.shape[0]])  36.6 us
    convert_element_type x1, local copies, waits for them, and re-layouts, reduce_gradients(): big.astype(bf16).reshape(8, 4, rows, 3, cols // 3).transpose(3, 1, 0, 2, 4)  31.2 us
    reshape x5, local copies, waits for them, and re-layouts, blocks_of(): full.reshape(rows_dp, rows // rows_dp, cols_ffn, cols // cols_ffn)  30.2 us
    transpose x7, local copies, waits for them, and re-layouts, columns(): return blocks.transpose(0, 2, 1, 3).reshape(rows_dp * rows, cols_ffn * cols)  23.9 us

profile of v2, /device:TPU:0, one launch (start us, length us, event | category | flops | bytes accessed | tf_op | source)
XLA Modules:
  0.0 633.1 jit_solution(7744974735851364685)
XLA Ops:
  2.7 1.4 fusion.67.small
  6.1 77.6 %gather_weights.1 = (bf16[3,4,768,768]{3,2,1,0:T(8,128)(2,1)}, bf16[4,1152,128]{2,1,0:T(8,128)(2,1)}) custom-call(bf16[3,96,768]{2,1,0:T(8,128)(2,1)} %bitcast.251, bf16[144,128]{1,0:T(8,128)(2,1)} %fusion.67.small), custom_call_target="tpu_custom_call" | custom-call | tf_op jit(solution)/shard_map/gather_weights/pallas_call | solution.py:197
  83.7 1.4 copy.135
  91.8 20.2 %copy.133 = bf16[3,4,8,96,768]{4,0,3,1,2:T(4,128)(2,1)} copy(bf16[3,4,8,96,768]{4,3,2,1,0:T(8,128)(2,1)} %bitcast.199) | data formatting | bytes 28311552 | tf_op jit(solution)/shard_map/reshape | solution.py:327
  112.0 36.6 %reshape.296 = bf16[8,4,96,2304]{3,2,1,0:T(8,128)(2,1)} reshape(bf16[8,4,96,3,768]{4,3,2,1,0:T(4,128)(2,1)} %bitcast.191) | data formatting | bytes 28311552 | tf_op jit(solution)/shard_map/reshape | solution.py:329
  148.6 2.4 slice_bitcast_fusion.3
  152.1 2.1 reshape.299
  154.2 2.5 slice_bitcast_fusion.2
  156.7 6.8 %slice_bitcast_fusion = (bf16[8,96,4,768]{3,1,2,0:T(8,128)(2,1)S(1)}, bf16[8,96,4,768]{3,1,2,0:T(8,128)(2,1)}) fusion(bf16[8,4,96,2304]{3,2,1,0:T(8,128)(2,1)} %reshape.296), kind=kLoop, calls=%fused_computation.55 | loop fusion | bytes 18874368 | tf_op jit(solution)/shard_map/transpose | solution.py:338
  163.5 3.6 copy.94
  167.1 3.3 copy.124
  170.4 3.9 copy.86
  174.3 8.1 %reshape.297 = bf16[768,2304]{1,0:T(8,128)(2,1)} reshape(bf16[8,96,4,576]{3,2,1,0:T(4,128)(2,1)} %copy.86) | data formatting | bytes 7077888 | tf_op jit(solution)/shard_map/reshape | solution.py:338
  182.4 6.8 %fusion.28 = bf16[1024,2304]{0,1:T(8,128)(2,1)S(1)} fusion(bf16[768,2304]{1,0:T(8,128)(2,1)} %reshape.297, bf16[1024,768]{1,0:T(8,128)(2,1)S(1)} %bitcast.263, f32[2304]{0:T(1024)S(1)} %pad_maximum_fusion.3), kind=kOutput, calls=%fused_computation.54 | convolution fusion | flops 3628597248 | bytes 9839616 | tf_op jit(solution)/shard_map/dot_general | solution.py:28
  189.2 1.6 fusion.79
  190.8 3.6 copy.93
  194.5 3.1 copy.123
  197.7 3.8 fusion.81
  201.5 1.9 fusion.17
  204.6 1.4 copy-done
  206.0 3.6 fusion.48
  209.7 3.8 fusion.82
  213.5 1.9 fusion.16
  216.0 3.2 copy-done.1
  219.2 3.8 fusion.49
  223.0 1.6 fusion.83
  225.3 34.7 %fusion.2 = (bf16[1024,3072]{1,0:T(8,128)(2,1)S(1)}, f32[1024,3072]{1,0:T(8,128)}) fusion(f32[3072]{0:T(1024)S(1)} %reshape.314, bf16[768,3072]{1,0:T(8,128)(2,1)S(1)} %bitcast.224, f32[1024,768]{1,0:T(8,128)S(1)} %get-tuple-element.62, f32[768]{0:T(1024)S(1)} %add.180, f32[768]{0:T(1024)S(1)} %mul.179, f32[1024]{0:T(1024)S(1)} %add_rsqrt_fusion.1, ...), kind=kOutput, calls=%fused_computation.5 | convolution fusion | flops 5043388416 | bytes 26765312 | tf_op jit(solution)/shard_map/dot_general | solution.py:28
  260.1 5.5 fusion.84
  267.4 3.6 fusion.76
  271.0 12.0 %convert_reduce_fusion = (f32[3072]{0:T(1024)S(1)}, bf16[1024,3072]{1,0:T(8,128)(2,1)S(1)}) fusion(f32[1024,3072]{1,0:T(8,128)} %get-tuple-element.64, f32[3072]{0:T(1024)S(1)} %reshape.314, bf16[768,3072]{1,0:T(8,128)(2,1)} %bitcast.218, f32[1024,768]{1,0:T(8,128)S(1)} %get-tuple-element.37), kind=kOutput, calls=%fused_computation.12 | convolution fusion | flops 4873516032 | bytes 26763264 | tf_op jit(solution)/shard_map/dot_general | solution.py:28
  283.0 7.3 %convolution_convert_fusion = bf16[768,3072]{1,0:T(8,128)(2,1)} fusion(bf16[1024,3072]{1,0:T(8,128)(2,1)S(1)} %bitcast.272, f32[1024,768]{1,0:T(8,128)S(1)} %get-tuple-element.37), kind=kOutput, calls=%fused_computation.51 | convolution fusion | flops 4834983936 | bytes 14155776 | tf_op jit(solution)/shard_map/dot_general | solution.py:20
  290.4 7.5 %multiply_reduce_fusion.2 = (f32[768]{0:T(1024)S(1)}, f32[1024]{0:T(1024)S(1)}, f32[1024]{0:T(1024)S(1)}, f32[768]{0:T(1024)S(1)}, f32[1024,768]{1,0:T(8,128)}) fusion(f32[1024,768]{1,0:T(8,128)S(1)} %copy-done.5, f32[1024]{0:T(1024)S(1)} %add_rsqrt_fusion.1, f32[1024]{0:T(1024)S(1)} %broadcast_multiply_fusion.4, f32[768]{0:T(1024)S(1)} %mul.179, ...), kind=kOutput, calls=%fused_computation.79 | convolution fusion | flops 4839698432 | bytes 20472832 | tf_op jit(solution)/shard_map/dot_general | solution.py:24
  298.0 9.8 %reshape.307 = bf16[8,96,4,768]{3,2,1,0:T(4,128)(2,1)} reshape(bf16[768,3072]{1,0:T(8,128)(2,1)} %convolution_convert_fusion) | data formatting | bytes 9437184 | tf_op jit(solution)/shard_map/reshape | solution.py:343
  309.1 2.6 fusion.78
  312.8 7.7 %convolution_convert_fusion.1 = bf16[768,3072]{1,0:T(8,128)(2,1)} fusion(bf16[1024,3072]{1,0:T(8,128)(2,1)S(1)} %copy-done.48, f32[1024,768]{1,0:T(8,128)S(1)} %copy-done.5, f32[768]{0:T(1024)S(1)} %add.180, f32[768]{0:T(1024)S(1)} %mul.179, f32[1024]{0:T(1024)S(1)} %add_rsqrt_fusion.1, f32[1024]{0:T(1024)S(1)} %broadcast_multiply_fusion.4), kind=kOutput, calls=%fused_computation.52 | convolution fusion | flops 4838129664 | bytes 14170112 | tf_op jit(solution)/shard_map/dot_general | solution.py:20
  320.6 2.4 convolution_convert_fusion.4
  323.6 9.9 %reshape.306 = bf16[8,96,4,768]{3,2,1,0:T(4,128)(2,1)} reshape(bf16[768,3072]{1,0:T(8,128)(2,1)} %convolution_convert_fusion.1) | data formatting | bytes 9437184 | tf_op jit(solution)/shard_map/reshape | solution.py:343
  333.6 9.3 %copy_bitcast_fusion.1 = (bf16[8,4,96,768]{3,2,1,0:T(8,128)(2,1)}, bf16[8,4,96,768]{3,2,1,0:T(8,128)(2,1)}) fusion(bf16[8,96,4,768]{3,2,1,0:T(4,128)(2,1)} %reshape.307, bf16[8,96,4,768]{3,2,1,0:T(4,128)(2,1)} %reshape.306), kind=kLoop, calls=%fused_computation.58 | loop fusion | bytes 18874368 | tf_op jit(solution)/shard_map/transpose | solution.py:343
  343.6 3.5 reshape.305
  347.0 1.4 copy.134
  348.5 3.5 convolution_convert_fusion.3
  352.1 7.0 %fusion.45 = bf16[12,64,512]{2,1,0:T(8,128)(2,1)S(1)} fusion(bf16[512,12,64]{0,2,1:T(8,128)(2,1)S(1)} %bitcast.200, f32[12,512,512]{1,2,0:T(8,128)} %copy-done, f32[12,512]{1,0:T(8,128)S(1)} %copy-done.30), kind=kOutput, calls=%fused_computation.107 | convolution fusion | flops 409337856 | bytes 14180352 | tf_op jit(solution)/shard_map/hqk,qhd->khd/dot_general | solution.py:79
  359.3 2.0 fusion.42
  363.2 8.8 %multiply_reduce_fusion.1 = (f32[12,512]{1,0:T(8,128)S(1)}, f32[12,512,512]{1,2,0:T(8,128)}) fusion(f32[12,512,512]{1,2,0:T(8,128)} %copy-done.1, f32[12,512]{1,0:T(8,128)S(1)} %copy-done.31, bf16[512,12,64]{0,2,1:T(8,128)(2,1)S(1)} %bitcast.203, bf16[512,12,64]{0,2,1:T(8,128)(2,1)S(1)} %bitcast.239), kind=kOutput, calls=%fused_computation.17 | convolution fusion | flops 412084224 | bytes 26787840 | tf_op jit(solution)/shard_map/qhd,khd->hqk/dot_general | solution.py:78
  372.1 12.1 %fusion.30 = (f32[512,512]{0,1:T(8,128)}, bf16[12,512,512]{1,2,0:T(8,128)(2,1)S(1)}) fusion(f32[12,512,512]{1,2,0:T(8,128)} %get-tuple-element.71, f32[12,512]{1,0:T(8,128)S(1)} %get-tuple-element.70, f32[12,512,512]{1,2,0:T(8,128)} %copy-done.1, f32[12,512]{1,0:T(8,128)S(1)} %copy-done.31), kind=kLoop, calls=%fused_computation.62 | loop fusion | flops 15466496 | bytes 32555008 | tf_op jit(solution)/shard_map/reduce_sum | solution.py:83
  384.1 2.9 multiply_convert_fusion.1
  387.0 2.1 multiply_convert_fusion.3
  389.1 4.3 multiply_reduce_fusion
  393.4 5.4 fusion.32
  399.0 1.3 copy.107
  400.3 2.6 add.200
  402.9 5.2 multiply_convert_fusion
  412.0 5.5 convolution_add_fusion.1
  417.8 29.4 %fusion.29 = bf16[768,2304]{0,1:T(8,128)(2,1)} fusion(bf16[1024,768]{1,0:T(8,128)(2,1)S(1)} %bitcast.265, bf16[512,768]{0,1:T(8,128)(2,1)S(1)} %bitcast.242, bf16[512,768]{0,1:T(8,128)(2,1)S(1)} %bitcast.245, bf16[512,768]{0,1:T(8,128)(2,1)S(1)} %bitcast.258, bf16[512,768]{0,1:T(8,128)(2,1)S(1)} %bitcast.256, bf16[512,768]{0,1:T(8,128)(2,1)S(1)} %bitcast.213, ...), kind=kOutput, calls=%fused_computation.60 | convolution fusion | flops 3653959680 | bytes 9830400 | tf_op jit(solution)/shard_map/dot_general | solution.py:20
  447.2 4.3 copy.101
  452.2 1.4 stack.35
  454.4 1.6 fusion.50
  457.4 5.6 reshape.304
  463.0 4.8 copy.105
  467.7 21.6 %concatenate.44 = bf16[8,4,96,2304]{3,2,1,0:T(8,128)(2,1)} concatenate(bf16[8,4,96,576]{3,2,1,0:T(8,128)(2,1)} %copy.105, bf16[8,4,96,192]{3,2,1,0:T(8,128)(2,1)S(1)} %bitcast.214, bf16[8,4,96,768]{3,2,1,0:T(8,128)(2,1)} %get-tuple-element.77, bf16[8,4,96,768]{3,2,1,0:T(8,128)(2,1)} %get-tuple-element.76), dimensions={3} | concatenate | bytes 28311552 | tf_op jit(solution)/shard_map/concatenate | solution.py:503
  489.3 31.2 %convert_element_type.247 = bf16[8,4,96,3,768]{4,3,2,1,0:T(4,128)(2,1)} reshape(bf16[8,4,96,2304]{3,2,1,0:T(8,128)(2,1)} %concatenate.44) | data formatting | bytes 28311552 | tf_op jit(solution)/shard_map/convert_element_type | solution.py:349
  520.6 16.1 %copy.106 = bf16[3,4,8,96,768]{4,3,2,1,0:T(8,128)(2,1)} copy(bf16[3,4,8,96,768]{4,0,3,1,2:T(4,128)(2,1)} %bitcast.192) | data formatting | bytes 28311552 | tf_op jit(solution)/shard_map/transpose | solution.py:349
  536.7 87.5 %reduce_gradients.1 = (f32[3,96,768]{2,1,0:T(8,128)}, f32[80,128]{1,0:T(8,128)}) custom-call(bf16[3,4,768,768]{3,2,1,0:T(8,128)(2,1)} %bitcast.193, f32[4,640,128]{2,1,0:T(8,128)} %bitcast.217), custom_call_target="tpu_custom_call" | custom-call | tf_op jit(solution)/shard_map/reduce_gradients/pallas_call | solution.py:308
  629.2 1.4 divide_multiply_fusion
  (207 shorter events, 35.8 us)
Async XLA Ops:
  85.0 4.7 copy-start.2
  88.0 24.0 %copy-start.32 = (f32[768]{0:T(1024)}, f32[768]{0:T(1024)S(1)}, u32[]{:S(2)}) copy-start(f32[768]{0:T(1024)S(1)} %mul.188) | copy-start | bytes 9220
  174.3 8.1 %copy-start.40 = (bf16[2,512,768]{2,1,0:T(8,128)(2,1)S(1)}, bf16[2,512,768]{2,1,0:T(8,128)(2,1)}, u32[]{:S(2)}) copy-start(bf16[2,512,768]{2,1,0:T(8,128)(2,1)} %param.13) | copy-start | bytes 4718596
  174.3 16.5 %slice-start.8 = ((s8[4718592]{0:T(1024)(128)(4,1)}), s8[524288]{0:T(1024)(128)(4,1)S(1)}, s32[]{:S(2)}) async-start(s8[4718592]{0:T(1024)(128)(4,1)} %bitcast.196), calls=%async_computation.8 | async-start | bytes 1048576
  182.4 8.4 %slice-start.9 = ((s8[4718592]{0:T(1024)(128)(4,1)}), s8[4194304]{0:T(1024)(128)(4,1)S(1)}, s32[]{:S(2)}) async-start(s8[4718592]{0:T(1024)(128)(4,1)} %bitcast.196), calls=%async_computation.9 | async-start | bytes 8388608
  190.8 6.9 %copy-start.7 = (bf16[512,768]{0,1:T(8,128)(2,1)}, bf16[512,768]{0,1:T(8,128)(2,1)S(1)}, u32[]{:S(2)}) copy-start(bf16[512,768]{0,1:T(8,128)(2,1)S(1)} %get-tuple-element.47) | copy-start | bytes 2359300
  190.8 13.8 %copy-start.15 = (bf16[512,768]{0,1:T(8,128)(2,1)}, bf16[512,768]{0,1:T(8,128)(2,1)S(1)}, u32[]{:S(2)}) copy-start(bf16[512,768]{0,1:T(8,128)(2,1)S(1)} %get-tuple-element.49) | copy-start | bytes 2359300
  190.8 18.9 %copy-start.9 = (bf16[512,768]{0,1:T(8,128)(2,1)}, bf16[512,768]{0,1:T(8,128)(2,1)S(1)}, u32[]{:S(2)}) copy-start(bf16[512,768]{0,1:T(8,128)(2,1)S(1)} %get-tuple-element.46) | copy-start | bytes 2359300
  194.5 3.2 copy-start.23
  194.5 3.2 copy-start.28
  201.5 4.5 copy-start
  206.0 3.7 copy-start.24
  213.5 5.7 copy-start.1
  213.5 11.7 %slice-start.12 = ((s8[4718592]{0:T(1024)(128)(4,1)}), s8[4194304]{0:T(1024)(128)(4,1)S(1)}, s32[]{:S(2)}) async-start(s8[4718592]{0:T(1024)(128)(4,1)} %bitcast.222), calls=%async_computation.12 | async-start | bytes 8388608
  219.2 3.8 copy-start.26
  219.2 3.8 copy-start.41
  219.2 3.8 copy-start.43
  219.2 6.0 slice-start.13
  223.0 37.0 %slice-start.10 = ((s8[4718592]{0:T(1024)(128)(4,1)}), s8[4194304]{0:T(1024)(128)(4,1)S(1)}, s32[]{:S(2)}) async-start(s8[4718592]{0:T(1024)(128)(4,1)} %bitcast.219), calls=%async_computation.10 | async-start | bytes 8388608
  224.7 35.3 %copy-start.4 = (f32[1024,768]{1,0:T(8,128)}, f32[1024,768]{1,0:T(8,128)S(1)}, u32[]{:S(2)}) copy-start(f32[1024,768]{1,0:T(8,128)S(1)} %get-tuple-element.62) | copy-start | bytes 9437188
  225.3 34.7 %slice-start.11 = ((s8[4718592]{0:T(1024)(128)(4,1)}), s8[524288]{0:T(1024)(128)(4,1)S(1)}, s32[]{:S(2)}) async-start(s8[4718592]{0:T(1024)(128)(4,1)} %bitcast.219), calls=%async_computation.11 | async-start | bytes 1048576
  225.3 34.7 %copy-start.39 = (f32[768]{0:T(1024)S(1)}, f32[768]{0:T(1024)}, u32[]{:S(2)}) copy-start(f32[768]{0:T(1024)} %add.186) | copy-start | bytes 9220
  260.0 5.6 copy-start.49
  260.0 6.0 copy-start.3
  260.0 6.0 copy-start.33
  265.5 1.8 copy-start.36
  267.4 15.6 %slice-start.16 = ((s8[6291456]{0:T(1024)(128)(4,1)}), s8[4194304]{0:T(1024)(128)(4,1)S(1)}, s32[]{:S(2)}) async-start(s8[6291456]{0:T(1024)(128)(4,1)} %bitcast.271), calls=%async_computation.16 | async-start | bytes 8388608
  267.4 23.0 %slice-start.14 = ((s8[4718592]{0:T(1024)(128)(4,1)}), s8[4194304]{0:T(1024)(128)(4,1)S(1)}, s32[]{:S(2)}) async-start(s8[4718592]{0:T(1024)(128)(4,1)} %bitcast.225), calls=%async_computation.14 | async-start | bytes 8388608
  271.0 12.0 %slice-start.17 = ((s8[6291456]{0:T(1024)(128)(4,1)}), s8[2097152]{0:T(1024)(128)(4,1)S(1)}, s32[]{:S(2)}) async-start(s8[6291456]{0:T(1024)(128)(4,1)} %bitcast.271), calls=%async_computation.17 | async-start | bytes 4194304
  271.0 19.4 %slice-start.15 = ((s8[4718592]{0:T(1024)(128)(4,1)}), s8[524288]{0:T(1024)(128)(4,1)S(1)}, s32[]{:S(2)}) async-start(s8[4718592]{0:T(1024)(128)(4,1)} %bitcast.225), calls=%async_computation.15 | async-start | bytes 1048576
  283.0 7.3 %copy-start.47 = (bf16[1024,3072]{1,0:T(8,128)(2,1)}, bf16[1024,3072]{1,0:T(8,128)(2,1)S(1)}, u32[]{:S(2)}) copy-start(bf16[1024,3072]{1,0:T(8,128)(2,1)S(1)} %get-tuple-element.73) | copy-start | bytes 18874372
  283.0 7.4 %copy-start.5 = (f32[1024,768]{1,0:T(8,128)S(1)}, f32[1024,768]{1,0:T(8,128)}, u32[]{:S(2)}) copy-start(f32[1024,768]{1,0:T(8,128)} %copy-done.4) | copy-start | bytes 9437188
  309.1 3.7 copy-start.48
  312.8 7.7 %copy-start.21 = (f32[1024,768]{1,0:T(8,128)}, f32[1024,768]{1,0:T(8,128)S(1)}, u32[]{:S(2)}) copy-start(f32[1024,768]{1,0:T(8,128)S(1)} %get-tuple-element.39) | copy-start | bytes 9437188
  312.8 7.7 %copy-start.44 = (bf16[12,64,512]{2,1,0:T(8,128)(2,1)S(1)}, bf16[12,64,512]{2,1,0:T(8,128)(2,1)}, u32[]{:S(2)}) copy-start(bf16[12,64,512]{2,1,0:T(8,128)(2,1)} %fusion.48) | copy-start | bytes 2359300
  312.8 7.7 %copy-start.46 = (bf16[12,64,512]{2,1,0:T(8,128)(2,1)S(1)}, bf16[12,64,512]{2,1,0:T(8,128)(2,1)}, u32[]{:S(2)}) copy-start(bf16[12,64,512]{2,1,0:T(8,128)(2,1)} %copy-done.45) | copy-start | bytes 2359300
  342.9 5.6 copy-start.27
  348.5 3.6 copy-start.30
  348.5 10.7 %slice-start.3 = ((s8[12582912]{0:T(1024)(128)(4,1)}), s8[4194304]{0:T(1024)(128)(4,1)S(1)}, s32[]{:S(2)}) async-start(s8[12582912]{0:T(1024)(128)(4,1)} %bitcast.187), calls=%async_computation.3 | async-start | bytes 8388608
  352.0 7.2 %slice-start.4 = ((s8[12582912]{0:T(1024)(128)(4,1)}), s8[4194304]{0:T(1024)(128)(4,1)S(1)}, s32[]{:S(2)}) async-start(s8[12582912]{0:T(1024)(128)(4,1)} %bitcast.187), calls=%async_computation.4 | async-start | bytes 8388608
  352.1 7.0 %copy-start.6 = (bf16[512,768]{0,1:T(8,128)(2,1)}, bf16[512,768]{0,1:T(8,128)(2,1)S(1)}, u32[]{:S(2)}) copy-start(bf16[512,768]{0,1:T(8,128)(2,1)S(1)} %get-tuple-element.54) | copy-start | bytes 2359300
  352.1 7.2 %slice-start.5 = ((s8[12582912]{0:T(1024)(128)(4,1)}), s8[4194304]{0:T(1024)(128)(4,1)S(1)}, s32[]{:S(2)}) async-start(s8[12582912]{0:T(1024)(128)(4,1)} %bitcast.187), calls=%async_computation.5 | async-start | bytes 8388608
  352.1 7.1 %copy-start.31 = (f32[12,512]{1,0:T(8,128)S(1)}, f32[12,512]{1,0:T(8,128)}, u32[]{:S(2)}) copy-start(f32[12,512]{1,0:T(8,128)} %log_add_fusion.1) | copy-start | bytes 73732
  359.1 2.2 copy-start.17
  359.3 3.9 copy-start.16
  372.0 12.1 %copy-start.25 = (bf16[512,768]{0,1:T(8,128)(2,1)S(1)}, bf16[512,768]{0,1:T(8,128)(2,1)}, u32[]{:S(2)}) copy-start(bf16[512,768]{0,1:T(8,128)(2,1)} %get-tuple-element.50) | copy-start | bytes 2359300
  372.1 17.0 %slice-start = ((s8[12582912]{0:T(1024)(128)(4,1)}), s8[4194304]{0:T(1024)(128)(4,1)S(1)}, s32[]{:S(2)}) async-start(s8[12582912]{0:T(1024)(128)(4,1)} %bitcast.185), calls=%async_computation | async-start | bytes 8388608
  372.1 17.0 %slice-start.1 = ((s8[12582912]{0:T(1024)(128)(4,1)}), s8[4194304]{0:T(1024)(128)(4,1)S(1)}, s32[]{:S(2)}) async-start(s8[12582912]{0:T(1024)(128)(4,1)} %bitcast.185), calls=%async_computation.1 | async-start | bytes 8388608
  384.1 2.9 copy-start.10
  384.1 5.0 slice-start.2
  393.4 5.4 copy-start.13
  399.0 9.1 %slice-start.6 = ((s8[6291456]{0:T(1024)(128)(4,1)}), s8[2097152]{0:T(1024)(128)(4,1)S(1)}, s32[]{:S(2)}) async-start(s8[6291456]{0:T(1024)(128)(4,1)} %bitcast.189), calls=%async_computation.6 | async-start | bytes 4194304
  400.3 7.8 %copy-start.8 = (bf16[512,768]{0,1:T(8,128)(2,1)S(1)}, bf16[512,768]{0,1:T(8,128)(2,1)}, u32[]{:S(2)}) copy-start(bf16[512,768]{0,1:T(8,128)(2,1)} %copy-done.7) | copy-start | bytes 2359300
  402.9 5.2 slice-start.7
  408.2 2.2 copy-start.14
  408.2 2.4 copy-start.18
  408.2 2.6 copy-start.20
  408.2 3.6 copy-start.22
  408.2 3.8 copy-start.29
  411.9 5.8 copy-start.42
  447.2 5.0 copy-start.38
  463.0 4.8 copy-start.12
  536.7 92.5 %copy-start.34 = (bf16[64,128]{1,0:T(8,128)(2,1)S(1)}, bf16[64,128]{1,0:T(8,128)(2,1)}, u32[]{:S(2)}) copy-start(bf16[64,128]{1,0:T(8,128)(2,1)} %param.23) | copy-start | bytes 49156
  536.7 92.5 %copy-start.35 = (bf16[64,128]{1,0:T(8,128)(2,1)S(1)}, bf16[64,128]{1,0:T(8,128)(2,1)}, u32[]{:S(2)}) copy-start(bf16[64,128]{1,0:T(8,128)(2,1)} %param.22) | copy-start | bytes 49156
  (4 other events, 5.6 us)
